TPU v7x, 32 devices: a whole 2x2x4 slice. The times are simulated.
32 devices in a mesh: img: 16 (over z, y, core), seq: 2 (over x).
Axes of the slice: x: 2, y: 2, z: 4, core: 2. Of those that a mesh axis runs over, the one named last changes fastest.
Arguments:
- patches: bfloat16 [96, 2, 160, 768], P('img', 'seq'), may hold values from -6 to 6
- grid_shape: int32 [96, 2], P('img'), may hold values from 8 to 24, as said below
- split_rows: int32 [96], P('img'), may hold values from 1 to 11, as said below
- owner_shard: int32 [96], P('img'), may hold values from 0 to 1
- drop_masks: int32 [96, 2], P('img'), may hold values 0 or 1
- ln1_gain: float32 [768], replicated, may hold values from 0.25 to 1.75
- ln1_bias: float32 [768], replicated, may hold values from -3 to 3
- qkv_weight: bfloat16 [768, 2304], replicated, may hold values from -0.21875 to 0.21875
- qv_bias: float32 [1536], replicated, may hold values from -3 to 3
- proj_weight: bfloat16 [768, 768], replicated, may hold values from -0.875 to 0.875
- proj_bias: float32 [768], replicated, may hold values from -3 to 3
- ln2_gain: float32 [768], replicated, may hold values from 0.25 to 1.75
- ln2_bias: float32 [768], replicated, may hold values from -3 to 3
- fc1_weight: bfloat16 [768, 3072], replicated, may hold values from -0.21875 to 0.21875
- fc1_bias: float32 [3072], replicated, may hold values from -3 to 3
- fc2_weight: bfloat16 [3072, 768], replicated, may hold values from -0.21875 to 0.21875
- fc2_bias: float32 [768], replicated, may hold values from -3 to 3
- cotangent: bfloat16 [96, 2, 160, 768], P('img', 'seq'), may hold values from -6 to 6
Outputs:
- layer_out: bfloat16 [96, 2, 160, 768], P('img', 'seq')
- patches_grad: float32 [96, 2, 160, 768], P('img', 'seq')
- ln1_gain_grad: float32 [768], P(('img', 'seq'))
- ln1_bias_grad: float32 [768], P(('img', 'seq'))
- qkv_weight_grad: float32 [768, 2304], P(('img', 'seq'))
- qv_bias_grad: float32 [1536], P(('img', 'seq'))
- proj_weight_grad: float32 [768, 768], P(('img', 'seq'))
- proj_bias_grad: float32 [768], P(('img', 'seq'))
- ln2_gain_grad: float32 [768], P(('img', 'seq'))
- ln2_bias_grad: float32 [768], P(('img', 'seq'))
- fc1_weight_grad: float32 [768, 3072], P(('img', 'seq'))
- fc1_bias_grad: float32 [3072], P(('img', 'seq'))
- fc2_weight_grad: float32 [3072, 768], P(('img', 'seq'))
- fc2_bias_grad: float32 [768], P(('img', 'seq'))
Inputs may be any that keep to these rules, and one draw needn't show every extreme that they name: `grid_shape`: column 0 is the height, from 8 to 20; column 1 is the width, min(24, 280 // height), so an image has at most 280 patches. `split_rows`: both parts of every image hold at least one and at most 158 patches.
All inputs are finite; a program needn't handle non-finite values. No bound on the sum of `drop_masks` on one device may be relied on, other than what follows from the above.
Results may differ from a plain program's by a relative error of at most 0.014.
Values may be sent and summed in bfloat16 or wider, within the bound.
A program may use at most 192 MiB of HBM per device.

v0:
```python
import functools

import jax
import jax.numpy as jnp
from jax import lax
from jax.experimental import pallas as pl
from jax.experimental.pallas import tpu as pltpu
from jax.sharding import PartitionSpec as P

HEAD_DIM = 64
LN_EPS = 1e-06
KEEP_SCALE = 1.0 / 0.9
MASK_FILL = -1e30
BF16 = jnp.bfloat16
F32 = jnp.float32
MIB = 1024 * 1024


def dot_nn(a, b):
    return lax.dot_general(a, b, (((1,), (0,)), ((), ())), preferred_element_type=F32)


def dot_nt(a, b):
    return lax.dot_general(a, b, (((1,), (1,)), ((), ())), preferred_element_type=F32)


def dot_tn(a, b):
    return lax.dot_general(a, b, (((0,), (0,)), ((), ())), preferred_element_type=F32)


def norm_parts(values):
    row_mean = jnp.mean(values, axis=-1, keepdims=True)
    centred = values - row_mean
    variance = jnp.mean(centred * centred, axis=-1, keepdims=True)
    rstd = lax.rsqrt(variance + LN_EPS)
    return centred * rstd, rstd


def norm_back(d_normed, gain, unit, rstd):
    d_unit = d_normed * gain
    mean_one = jnp.mean(d_unit, axis=-1, keepdims=True)
    mean_two = jnp.mean(d_unit * unit, axis=-1, keepdims=True)
    return rstd * (d_unit - mean_one - unit * mean_two)


def gelu_both(values):
    size = jnp.abs(values)
    t = 1.0 / (1.0 + 0.23164189 * size)
    bell = jnp.exp(-0.5 * values * values)
    poly = t * (
        0.127414796
        + t * (-0.142248368 + t * (0.7107068705 + t * (-0.7265760135 + t * 0.5307027145)))
    )
    tail = poly * bell
    cdf = jnp.where(values >= 0.0, 1.0 - tail, tail)
    return values * cdf, cdf + values * (0.3989422804014327 * bell)


def row_valid(scal_ref, image, rows, half, axis):
    shape = (rows, 1) if axis == 0 else (1, rows)
    slot = lax.broadcasted_iota(jnp.int32, shape, axis)
    other = slot >= half
    place = jnp.where(other, slot - half, slot)
    count = jnp.where(other, scal_ref[image, 2], scal_ref[image, 0])
    special = jnp.where(other, scal_ref[image, 3], scal_ref[image, 1])
    return jnp.where(place < 2, special, (place - 2 < count).astype(jnp.int32)) > 0


def front_kernel(
    scal_ref, own_ref, oth_ref, g1_ref, b1_ref, wqkv_ref, qb_ref, vb_ref, wp_ref, pb_ref, g2_ref, b2_ref,
    n1_ref, qkv_ref, probs_ref, att_ref, mid_ref, n2_ref,
):
    image = pl.program_id(0)
    half, width = own_ref.shape[1], own_ref.shape[2]
    rows = 2 * half
    x = jnp.concatenate([own_ref[0].astype(F32), oth_ref[0].astype(F32)], axis=0)
    unit, _ = norm_parts(x)
    n1 = (unit * g1_ref[...] + b1_ref[...]).astype(BF16)
    n1_ref[0] = n1
    qkv_ref[0, :, :width] = ((dot_nn(n1, wqkv_ref[:, :width]) + qb_ref[...]).astype(BF16) * BF16(HEAD_DIM**-0.5))
    qkv_ref[0, :, width : 2 * width] = dot_nn(n1, wqkv_ref[:, width : 2 * width]).astype(BF16)
    qkv_ref[0, :, 2 * width :] = (dot_nn(n1, wqkv_ref[:, 2 * width :]) + vb_ref[...]).astype(BF16)
    fill = jnp.where(row_valid(scal_ref, image, rows, half, 1), 0.0, MASK_FILL)
    low_lane = lax.broadcasted_iota(jnp.int32, (rows, 128), 1) < HEAD_DIM
    for pair in range(width // 128):
        cut = slice(128 * pair, 128 * pair + 128)
        q2 = qkv_ref[0, :, cut]
        k2 = qkv_ref[0, :, width + 128 * pair : width + 128 * pair + 128]
        v2 = qkv_ref[0, :, 2 * width + 128 * pair : 2 * width + 128 * pair + 128]
        total = None
        for side in range(2):
            mine = low_lane if side == 0 else jnp.logical_not(low_lane)
            scores = dot_nt(jnp.where(mine, q2, 0), k2) + fill
            top = jnp.max(scores, axis=-1, keepdims=True)
            weight = jnp.exp(scores - top)
            probs = (weight * (1.0 / jnp.sum(weight, axis=-1, keepdims=True))).astype(BF16)
            probs_ref[0, 2 * pair + side] = probs
            part = dot_nn(probs, jnp.where(mine, v2, 0))
            total = part if total is None else total + part
        att_ref[0, :, cut] = total.astype(BF16)
    keep = scal_ref[image, 4].astype(F32) * KEEP_SCALE
    branch = dot_nn(att_ref[0], wp_ref[...]) + pb_ref[...]
    middle = jnp.concatenate([own_ref[0].astype(F32), oth_ref[0].astype(F32)], axis=0) + keep * branch
    mid_ref[0] = middle
    unit, _ = norm_parts(middle)
    n2_ref[0] = (unit * g2_ref[...] + b2_ref[...]).astype(BF16)


def full(shape):
    zeros = (0,) * len(shape)
    return pl.BlockSpec(shape, lambda *_: zeros, pipeline_mode=pl.Buffered(1))


def front(scal, own, oth, w):
    images, half, width = own.shape
    rows = 2 * half
    heads = width // HEAD_DIM
    per = lambda *tail: pl.BlockSpec((1,) + tail, lambda i, s: (i,) + (0,) * len(tail))
    flops = 2 * images * rows * width * (4 * width + 4 * rows)
    return pl.pallas_call(
        front_kernel,
        grid_spec=pltpu.PrefetchScalarGridSpec(
            num_scalar_prefetch=1,
            grid=(images,),
            in_specs=[
                per(half, width), per(half, width), full((1, width)), full((1, width)),
                full((width, 3 * width)), full((1, width)), full((1, width)),
                full((width, width)), full((1, width)), full((1, width)), full((1, width)),
            ],
            out_specs=[
                per(rows, width), per(rows, 3 * width), per(heads, rows, rows),
                per(rows, width), per(rows, width), per(rows, width),
            ],
        ),
        out_shape=[
            jax.ShapeDtypeStruct((images, rows, width), BF16),
            jax.ShapeDtypeStruct((images, rows, 3 * width), BF16),
            jax.ShapeDtypeStruct((images, heads, rows, rows), BF16),
            jax.ShapeDtypeStruct((images, rows, width), BF16),
            jax.ShapeDtypeStruct((images, rows, width), F32),
            jax.ShapeDtypeStruct((images, rows, width), BF16),
        ],
        compiler_params=pltpu.CompilerParams(vmem_limit_bytes=56 * MIB),
        cost_estimate=pl.CostEstimate(flops=flops, transcendentals=images * heads * rows * rows, bytes_accessed=30_000_000),
        name="front",
    )(scal, own, oth, w["ln1_gain"], w["ln1_bias"], w["qkv_weight"], w["q_bias"], w["v_bias"],
      w["proj_weight"], w["proj_bias"], w["ln2_gain"], w["ln2_bias"])


def mlp_kernel(
    scal_ref, n2_ref, mid_ref, w1_ref, c1_ref, w2_ref, c2_ref,
    hid_ref, slope_ref, own_ref, oth_ref, acc_ref,
):
    step = pl.program_id(0)
    images, half, width = own_ref.shape
    rows = 2 * half
    hidden, slope = gelu_both(dot_nn(n2_ref[...], w1_ref[...]) + c1_ref[...])
    hidden = hidden.astype(BF16)
    hid_ref[...] = hidden
    slope_ref[...] = slope.astype(BF16)
    part = dot_nn(hidden, w2_ref[...])

    @pl.when(step == 0)
    def _():
        acc_ref[...] = part

    @pl.when(step > 0)
    def _():
        acc_ref[...] += part

    @pl.when(step == pl.num_programs(0) - 1)
    def _():
        for image in range(images):
            keep = scal_ref[image, 5].astype(F32) * KEEP_SCALE
            cut = slice(rows * image, rows * image + rows)
            final = mid_ref[cut, :] + keep * (acc_ref[cut, :] + c2_ref[...])
            out = jnp.where(row_valid(scal_ref, image, rows, half, 0), final, 0.0).astype(BF16)
            own_ref[image] = out[:half]
            oth_ref[image] = out[half:]


def mlp(scal, n2, middle, w, images, tile):
    tokens, width = n2.shape
    hidden_width = w["fc1_weight"].shape[1]
    half = tokens // images // 2
    return pl.pallas_call(
        mlp_kernel,
        grid_spec=pltpu.PrefetchScalarGridSpec(
            num_scalar_prefetch=1,
            grid=(hidden_width // tile,),
            in_specs=[
                full((tokens, width)), full((tokens, width)),
                pl.BlockSpec((width, tile), lambda j, s: (0, j)), pl.BlockSpec((1, tile), lambda j, s: (0, j)),
                pl.BlockSpec((tile, width), lambda j, s: (j, 0)), full((1, width)),
            ],
            out_specs=[
                pl.BlockSpec((tokens, tile), lambda j, s: (0, j)), pl.BlockSpec((tokens, tile), lambda j, s: (0, j)),
                full((images, half, width)), full((images, half, width)),
            ],
            scratch_shapes=[pltpu.VMEM((tokens, width), F32)],
        ),
        out_shape=[
            jax.ShapeDtypeStruct((tokens, hidden_width), BF16),
            jax.ShapeDtypeStruct((tokens, hidden_width), BF16),
            jax.ShapeDtypeStruct((images, half, width), BF16),
            jax.ShapeDtypeStruct((images, half, width), BF16),
        ],
        compiler_params=pltpu.CompilerParams(vmem_limit_bytes=56 * MIB),
        cost_estimate=pl.CostEstimate(flops=4 * tokens * width * hidden_width, transcendentals=2 * tokens * hidden_width, bytes_accessed=30_000_000),
        name="mlp",
    )(scal, n2, middle, w["fc1_weight"], w["fc1_bias"], w["fc2_weight"], w["fc2_bias"])


def put_rows(grad_ref, value, send_ref, keep_ref, mine, lead):
    grad_ref[...] = value
    run = 2 * send_ref.shape[-2]
    for k in range(grad_ref.shape[0] // (2 * run)):
        for ref, core in ((send_ref, 1 - mine), (keep_ref, mine)):
            for x in range(2):
                at = pl.multiple_of((2 * k + core) * run + x * (run // 2), 8)
                ref[lead + (k, x)] = grad_ref[pl.ds(at, run // 2), :].astype(BF16)


def put_folded(grad_ref, value, send_ref, keep_ref, mine):
    grad_ref[...] = value
    unit = send_ref.shape[-2] // 2
    side = grad_ref.shape[1] // 2
    for k in range(grad_ref.shape[0] // (4 * unit)):
        for ref, core in ((send_ref, 1 - mine), (keep_ref, mine)):
            for x in range(2):
                at = pl.multiple_of((4 * k + 2 * core + x) * unit, 8)
                piece = grad_ref[pl.ds(at, unit), :]
                ref[k, x] = jnp.concatenate([piece[:, :side], piece[:, side:]], axis=0).astype(BF16)


def mlp_back_kernel(
    scal_ref, mine_ref, own_ref, oth_ref, n2_ref, hid_ref, slope_ref, w1_ref, w2_ref,
    dn2_ref, s2_ref, k2_ref, s1_ref, k1_ref, c2_ref, c1_ref, dmlp_ref, grad_ref, acc_ref,
):
    step = pl.program_id(0)
    images, half, width = own_ref.shape
    rows = 2 * half
    mine = mine_ref[0]

    @pl.when(step == 0)
    def _():
        total = jnp.zeros((1, width), F32)
        for image in range(images):
            keep = scal_ref[image, 5].astype(F32) * KEEP_SCALE
            cot = jnp.concatenate([own_ref[image].astype(F32), oth_ref[image].astype(F32)], axis=0)
            live = row_valid(scal_ref, image, rows, half, 0)
            d_mlp = (jnp.where(live, cot, 0.0) * keep).astype(BF16)
            dmlp_ref[rows * image : rows * image + rows, :] = d_mlp
            total += jnp.sum(d_mlp.astype(F32), axis=0, keepdims=True)
        c2_ref[...] = total

    d_pre = slope_ref[...].astype(F32) * dot_nt(dmlp_ref[...], w2_ref[...])
    d_pre = d_pre.astype(BF16)
    c1_ref[...] = jnp.sum(d_pre.astype(F32), axis=0, keepdims=True)
    part = dot_nt(d_pre, w1_ref[...])
    put_folded(grad_ref, dot_tn(n2_ref[...], d_pre), s1_ref, k1_ref, mine)
    put_rows(grad_ref, dot_tn(hid_ref[...], dmlp_ref[...]), s2_ref, k2_ref, mine, (0,))

    @pl.when(step == 0)
    def _():
        acc_ref[...] = part

    @pl.when(step > 0)
    def _():
        acc_ref[...] += part

    @pl.when(step == pl.num_programs(0) - 1)
    def _():
        dn2_ref[...] = acc_ref[...]


def mlp_back(scal, mine, own, oth, n2, hidden, slope, w, unit1, unit2):
    tokens, width = n2.shape
    images, half, _ = own.shape
    hidden_width = hidden.shape[1]
    tile = width
    steps = hidden_width // tile
    runs1, runs2 = width // (4 * unit1), tile // (4 * unit2)
    col = pl.BlockSpec((tokens, tile), lambda j, s, m: (0, j))
    half1 = pl.BlockSpec((runs1, 2, 2 * unit1, tile // 2), lambda j, s, m: (0, 0, 0, j))
    half2 = pl.BlockSpec((1, runs2, 2, unit2, width), lambda j, s, m: (j, 0, 0, 0, 0))
    return pl.pallas_call(
        mlp_back_kernel,
        grid_spec=pltpu.PrefetchScalarGridSpec(
            num_scalar_prefetch=2,
            grid=(steps,),
            in_specs=[
                full((images, half, width)), full((images, half, width)), full((tokens, width)), col, col,
                pl.BlockSpec((width, tile), lambda j, s, m: (0, j)), pl.BlockSpec((tile, width), lambda j, s, m: (j, 0)),
            ],
            out_specs=[
                full((tokens, width)), half2, half2, half1, half1,
                full((1, width)), pl.BlockSpec((1, tile), lambda j, s, m: (0, j)),
            ],
            scratch_shapes=[
                pltpu.VMEM((tokens, width), BF16), pltpu.VMEM((width, width), F32), pltpu.VMEM((tokens, width), F32),
            ],
        ),
        out_shape=[
            jax.ShapeDtypeStruct((tokens, width), F32),
            jax.ShapeDtypeStruct((steps, runs2, 2, unit2, width), BF16),
            jax.ShapeDtypeStruct((steps, runs2, 2, unit2, width), BF16),
            jax.ShapeDtypeStruct((runs1, 2, 2 * unit1, hidden_width // 2), BF16),
            jax.ShapeDtypeStruct((runs1, 2, 2 * unit1, hidden_width // 2), BF16),
            jax.ShapeDtypeStruct((1, width), F32),
            jax.ShapeDtypeStruct((1, hidden_width), F32),
        ],
        compiler_params=pltpu.CompilerParams(vmem_limit_bytes=58 * MIB),
        cost_estimate=pl.CostEstimate(flops=8 * tokens * width * hidden_width, transcendentals=0, bytes_accessed=35_000_000),
        name="mlp_back",
    )(scal, mine, own, oth, n2, hidden, slope, w["fc1_weight"], w["fc2_weight"])


def attend_back_kernel(
    scal_ref, own_ref, oth_ref, dn2_ref, mid_ref, qkv_ref, probs_ref, wp_ref, g2_ref,
    dmid_ref, dbr_ref, djoin_ref, g2g_ref, g2b_ref, pbg_ref, qbg_ref, vbg_ref, datt_ref,
):
    image = pl.program_id(0)
    half, width = own_ref.shape[1], own_ref.shape[2]
    rows = 2 * half
    live = row_valid(scal_ref, image, rows, half, 0)
    d_final = jnp.where(live, jnp.concatenate([own_ref[0].astype(F32), oth_ref[0].astype(F32)], axis=0), 0.0)
    unit, rstd = norm_parts(mid_ref[0])
    dn2 = dn2_ref[0]
    gain_part = jnp.sum(dn2 * unit, axis=0, keepdims=True)
    bias_part = jnp.sum(dn2, axis=0, keepdims=True)
    d_middle = d_final + norm_back(dn2, g2_ref[...], unit, rstd)
    dmid_ref[0] = d_middle
    keep = scal_ref[image, 4].astype(F32) * KEEP_SCALE
    d_branch = (d_middle * keep).astype(BF16)
    dbr_ref[0] = d_branch
    proj_part = jnp.sum(d_branch.astype(F32), axis=0, keepdims=True)
    datt_ref[...] = dot_nt(d_branch, wp_ref[...]).astype(BF16)
    low_lane = lax.broadcasted_iota(jnp.int32, (rows, 128), 1) < HEAD_DIM
    for pair in range(width // 128):
        cut = slice(128 * pair, 128 * pair + 128)
        q2 = qkv_ref[0, :, cut]
        k2 = qkv_ref[0, :, width + 128 * pair : width + 128 * pair + 128]
        v2 = qkv_ref[0, :, 2 * width + 128 * pair : 2 * width + 128 * pair + 128]
        a2 = datt_ref[:, cut]
        dq = dk = dv = None
        for side in range(2):
            mine = low_lane if side == 0 else jnp.logical_not(low_lane)
            probs_low = probs_ref[0, 2 * pair + side]
            probs = probs_low.astype(F32)
            a_side = jnp.where(mine, a2, 0)
            d_probs = dot_nt(a_side, v2)
            inner = jnp.sum(probs * d_probs, axis=-1, keepdims=True)
            d_scores = (probs * (d_probs - inner)).astype(BF16)
            dq_part = dot_nn(d_scores, jnp.where(mine, k2, 0))
            dk_part = dot_tn(d_scores, jnp.where(mine, q2, 0))
            dv_part = dot_tn(probs_low, a_side)
            dq = dq_part if dq is None else dq + dq_part
            dk = dk_part if dk is None else dk + dk_part
            dv = dv_part if dv is None else dv + dv_part
        djoin_ref[0, :, cut] = (dq * HEAD_DIM**-0.5).astype(BF16)
        djoin_ref[0, :, width + 128 * pair : width + 128 * pair + 128] = dk.astype(BF16)
        djoin_ref[0, :, 2 * width + 128 * pair : 2 * width + 128 * pair + 128] = dv.astype(BF16)
    q_part = jnp.sum(djoin_ref[0, :, :width].astype(F32), axis=0, keepdims=True)
    v_part = jnp.sum(djoin_ref[0, :, 2 * width :].astype(F32), axis=0, keepdims=True)
    sums = ((g2g_ref, gain_part), (g2b_ref, bias_part), (pbg_ref, proj_part), (qbg_ref, q_part), (vbg_ref, v_part))

    @pl.when(image == 0)
    def _():
        for ref, part in sums:
            ref[...] = part

    @pl.when(image > 0)
    def _():
        for ref, part in sums:
            ref[...] += part


def attend_back(scal, own, oth, dn2, middle, qkv, probs, w):
    images, half, width = own.shape
    rows = 2 * half
    heads = width // HEAD_DIM
    per = lambda *tail: pl.BlockSpec((1,) + tail, lambda i, s: (i,) + (0,) * len(tail))
    vec = jax.ShapeDtypeStruct((1, width), F32)
    return pl.pallas_call(
        attend_back_kernel,
        grid_spec=pltpu.PrefetchScalarGridSpec(
            num_scalar_prefetch=1,
            grid=(images,),
            in_specs=[
                per(half, width), per(half, width), per(rows, width), per(rows, width), per(rows, 3 * width),
                per(heads, rows, rows), full((width, width)), full((1, width)),
            ],
            out_specs=[per(rows, width), per(rows, width), per(rows, 3 * width)] + [full((1, width))] * 5,
            scratch_shapes=[pltpu.VMEM((rows, width), BF16)],
        ),
        out_shape=[
            jax.ShapeDtypeStruct((images, rows, width), F32),
            jax.ShapeDtypeStruct((images, rows, width), BF16),
            jax.ShapeDtypeStruct((images, rows, 3 * width), BF16),
            vec, vec, vec, vec, vec,
        ],
        compiler_params=pltpu.CompilerParams(vmem_limit_bytes=56 * MIB),
        cost_estimate=pl.CostEstimate(flops=2 * images * rows * width * (width + 8 * rows), transcendentals=0, bytes_accessed=35_000_000),
        name="attend_back",
    )(scal, own, oth, dn2, middle, qkv, probs, w["proj_weight"], w["ln2_gain"])


def tail_kernel(
    mine_ref, n1_ref, djoin_ref, att_ref, dbr_ref, wqkv_ref, xo_ref, xt_ref, dmid_ref, g1_ref,
    send_ref, keep_ref, go_ref, gt_ref, g1g_ref, g1b_ref, grad_ref, acc_ref,
):
    step = pl.program_id(0)
    last = pl.num_programs(0) - 1
    images, half, width = xo_ref.shape
    rows = 2 * half
    mine = mine_ref[0]

    @pl.when(step < last)
    def _():
        put_folded(grad_ref, dot_tn(n1_ref[...], djoin_ref[...]), send_ref, keep_ref, mine)
        part = dot_nt(djoin_ref[...], wqkv_ref[...])

        @pl.when(step == 0)
        def _():
            acc_ref[...] = part

        @pl.when(step > 0)
        def _():
            acc_ref[...] += part

    @pl.when(step == last)
    def _():
        put_folded(grad_ref, dot_tn(att_ref[...], dbr_ref[...]), send_ref, keep_ref, mine)
        gain_sum = jnp.zeros((1, width), F32)
        bias_sum = jnp.zeros((1, width), F32)
        for image in range(images):
            x = jnp.concatenate([xo_ref[image].astype(F32), xt_ref[image].astype(F32)], axis=0)
            unit, rstd = norm_parts(x)
            dn1 = acc_ref[rows * image : rows * image + rows, :]
            gain_sum += jnp.sum(dn1 * unit, axis=0, keepdims=True)
            bias_sum += jnp.sum(dn1, axis=0, keepdims=True)
            out = dmid_ref[rows * image : rows * image + rows, :] + norm_back(dn1, g1_ref[...], unit, rstd)
            go_ref[image] = out[:half]
            gt_ref[image] = out[half:].astype(BF16)
        g1g_ref[...] = gain_sum
        g1b_ref[...] = bias_sum


def tail(mine, n1, d_join, attended, d_branch, own, oth, d_middle, w, unit):
    tokens, width = n1.shape
    images, half, _ = own.shape
    runs = width // (4 * unit)
    halves = pl.BlockSpec((runs, 2, 2 * unit, width // 2), lambda j, m: (0, 0, 0, j))
    clip = lambda j: jnp.minimum(j, 2)
    return pl.pallas_call(
        tail_kernel,
        grid_spec=pltpu.PrefetchScalarGridSpec(
            num_scalar_prefetch=1,
            grid=(4,),
            in_specs=[
                full((tokens, width)), pl.BlockSpec((tokens, width), lambda j, m: (0, clip(j))), full((tokens, width)),
                full((tokens, width)), pl.BlockSpec((width, width), lambda j, m: (0, clip(j))),
                full((images, half, width)), full((images, half, width)), full((tokens, width)), full((1, width)),
            ],
            out_specs=[
                halves, halves, full((images, half, width)), full((images, half, width)),
                full((1, width)), full((1, width)),
            ],
            scratch_shapes=[pltpu.VMEM((width, width), F32), pltpu.VMEM((tokens, width), F32)],
        ),
        out_shape=[
            jax.ShapeDtypeStruct((runs, 2, 2 * unit, 2 * width), BF16),
            jax.ShapeDtypeStruct((runs, 2, 2 * unit, 2 * width), BF16),
            jax.ShapeDtypeStruct((images, half, width), F32),
            jax.ShapeDtypeStruct((images, half, width), BF16),
            jax.ShapeDtypeStruct((1, width), F32),
            jax.ShapeDtypeStruct((1, width), F32),
        ],
        compiler_params=pltpu.CompilerParams(vmem_limit_bytes=56 * MIB),
        cost_estimate=pl.CostEstimate(flops=14 * tokens * width * width, transcendentals=0, bytes_accessed=35_000_000),
        name="tail",
    )(mine, n1, d_join, attended, d_branch, w["qkv_weight"], own, oth, d_middle, w["ln1_gain"])


MESH = pl.DeviceIdType.MESH
DEPTH, LEVELS = 4, 2
PARTS = 6
GROUP = 32


def reduce_kernel(
    s2_ref, k2_ref, s1_ref, k1_ref, st_ref, kt_ref, small_ref,
    fc2_ref, fc1_ref, qkv_ref, proj_ref, tiny_ref,
    keep_ref, rc_ref, ra_ref, rb_ref, rz_ref, keep_t, rc_t, ra_t, rb_t, rz_t, load_sem, send_sem, recv_sem,
):
    line = lax.axis_index("img")
    x = lax.axis_index("seq")
    core = line % 2
    y = (line // 2) % 2
    z = line // 4
    sibling = (line + 1 - 2 * core, x)
    level = (line + 2 - 4 * y, x)
    across = (line, 1 - x)
    deep = [(((z + d) % DEPTH) * 4 + y * 2 + core, x) for d in range(1, DEPTH)]
    peers = [sibling, level, across] + deep
    barrier = pltpu.get_barrier_semaphore()
    for peer in peers:
        pl.semaphore_signal(barrier, inc=1, device_id=peer, device_id_type=MESH)
    pl.semaphore_wait(barrier, len(peers))

    rows, cols = keep_ref.shape[-2], keep_ref.shape[-1]
    pick = []
    for k in range(2):
        pick.append((s2_ref.at[:, :, :, pl.ds(k * rows, rows), :], k2_ref.at[:, :, :, pl.ds(k * rows, rows), :]))
    for s_ref, k_ref in ((s1_ref, k1_ref), (st_ref, kt_ref)):
        for k in range(2):
            pick.append((s_ref.at[:, :, :, :, pl.ds(k * cols, cols)], k_ref.at[:, :, :, :, pl.ds(k * cols, cols)]))

    def far(src, dst, part, slot, peer):
        copy = pltpu.make_async_remote_copy(
            src_ref=src, dst_ref=dst, send_sem=send_sem.at[part, slot], recv_sem=recv_sem.at[part, slot],
            device_id=peer, device_id_type=MESH,
        )
        copy.start()
        return copy

    pending = {}
    loads = []
    for part, (send, keep) in enumerate(pick):
        pending[part] = far(send, rc_ref.at[part], part, 0, sibling)
        load = pltpu.make_async_copy(keep, keep_ref.at[part], load_sem.at[part])
        load.start()
        loads.append(load)
    keep_t[...] = small_ref[:, :, pl.ds(core, 1)].reshape(keep_t.shape)
    pending[PARTS] = far(small_ref.at[:, :, 1 - core], rc_t, PARTS, 0, sibling)

    def add(target, source):
        target[...] = (target[...].astype(F32) + source[...].astype(F32)).astype(target.dtype)

    def stage_one(part, kept, rc, ra, first_level):
        pending[part].wait()
        if part < PARTS:
            loads[part].wait()

        @pl.loop(0, DEPTH * 2)
        def _(i):
            a, b = i // 2, i % 2
            for c in range(2):
                add(kept.at[a, b, c], rc.at[a, b, c])

        src = kept.at[:, 1 - y] if first_level else kept.at[:, :, 1 - x]
        pending[part] = far(src, ra, part, 1, level if first_level else across)

    def stage_two(part, kept, ra, rb, first_level):
        pending[part].wait()

        @pl.loop(0, DEPTH * 2)
        def _(i):
            a, b = i // 2, i % 2
            add(kept.at[a, y, b] if first_level else kept.at[a, b, x], ra.at[a, b])

        src = kept.at[:, y, 1 - x] if first_level else kept.at[:, 1 - y, x]
        pending[part] = far(src, rb, part, 2, across if first_level else level)

    def stage_three(part, kept, rb, rz):
        pending[part].wait()

        @pl.loop(0, DEPTH)
        def _(a):
            add(kept.at[a, y, x], rb.at[a])

        pending[part] = [
            far(kept.at[(z + d) % DEPTH, y, x], rz.at[d - 1], part, 2 + d, deep[d - 1]) for d in range(1, DEPTH)
        ]

    def stage_four(part, kept, rz):
        for copy in pending[part]:
            copy.wait()
        total = kept[z, y, x].astype(F32)
        for d in range(DEPTH - 1):
            total += rz[d].astype(F32)
        return total

    for part in range(PARTS):
        stage_one(part, keep_ref.at[part], rc_ref.at[part], ra_ref.at[part], part % 2 == 0)
    stage_one(PARTS, keep_t, rc_t, ra_t, True)
    for part in range(PARTS):
        stage_two(part, keep_ref.at[part], ra_ref.at[part], rb_ref.at[part], part % 2 == 0)
    stage_two(PARTS, keep_t, ra_t, rb_t, True)
    for part in range(PARTS):
        stage_three(part, keep_ref.at[part], rb_ref.at[part], rz_ref.at[part])
    stage_three(PARTS, keep_t, rb_t, rz_t)
    unit, side = rows // 2, cols // 2
    for part in range(PARTS):
        total = stage_four(part, keep_ref.at[part], rz_ref.at[part])
        if part < 2:
            fc2_ref[part * rows : part * rows + rows, :] = total
            continue
        for t in range(2):
            for h in range(2):
                piece = total[h * unit : h * unit + unit, t * side : t * side + side]
                at = ((part % 2) * 2 + t) * cols + h * side
                if part < 4:
                    fc1_ref[:, at : at + side] = piece
                elif at < 3 * cols:
                    qkv_ref[:, at : at + side] = piece
                else:
                    proj_ref[:, at - 3 * cols : at - 3 * cols + side] = piece
    tiny_ref[...] = stage_four(PARTS, keep_t, rz_t)


def reduce_all(s2, k2, s1, k1, st, kt, small):
    rows, cols = s1.shape[-2], s1.shape[-1] // 2
    unit = rows // 2
    s2, k2 = s2.reshape(DEPTH, 2, 2, 2 * rows, cols), k2.reshape(DEPTH, 2, 2, 2 * rows, cols)
    s1, k1, st, kt = (v.reshape(DEPTH, 2, 2, rows, 2 * cols) for v in (s1, k1, st, kt))
    small = small.reshape(DEPTH, 2, 2, 2, 8, 128)
    hbm = pl.BlockSpec(memory_space=pl.ANY)
    vmem = pl.BlockSpec(memory_space=pltpu.VMEM)
    return pl.pallas_call(
        reduce_kernel,
        in_specs=[hbm] * 6 + [vmem],
        out_specs=[vmem] * 5,
        out_shape=[
            jax.ShapeDtypeStruct((2 * rows, cols), F32),
            jax.ShapeDtypeStruct((unit, 4 * cols), F32),
            jax.ShapeDtypeStruct((unit, 3 * cols), F32),
            jax.ShapeDtypeStruct((unit, cols), F32),
            jax.ShapeDtypeStruct((8, 128), F32),
        ],
        scratch_shapes=[
            pltpu.VMEM((PARTS, DEPTH, 2, 2, rows, cols), BF16),
            pltpu.VMEM((PARTS, DEPTH, 2, 2, rows, cols), BF16),
            pltpu.VMEM((PARTS, DEPTH, 2, rows, cols), BF16),
            pltpu.VMEM((PARTS, DEPTH, rows, cols), BF16),
            pltpu.VMEM((PARTS, DEPTH - 1, rows, cols), BF16),
            pltpu.VMEM((DEPTH, 2, 2, 8, 128), F32),
            pltpu.VMEM((DEPTH, 2, 2, 8, 128), F32),
            pltpu.VMEM((DEPTH, 2, 8, 128), F32),
            pltpu.VMEM((DEPTH, 8, 128), F32),
            pltpu.VMEM((DEPTH - 1, 8, 128), F32),
            pltpu.SemaphoreType.DMA((PARTS,)),
            pltpu.SemaphoreType.DMA((PARTS + 1, 6)),
            pltpu.SemaphoreType.DMA((PARTS + 1, 6)),
        ],
        compiler_params=pltpu.CompilerParams(collective_id=0, has_side_effects=True, vmem_limit_bytes=48 * MIB),
        name="reduce",
    )(s2, k2, s1, k1, st, kt, small)


def spread(value):
    return lax.psum_scatter(value, ("img", "seq"), scatter_dimension=0, tiled=True)


def unfold(send, keep, core, folds):
    rows, cols = send.shape[-2], send.shape[-1]
    send, keep = (v.reshape(GROUP // 4, 2, rows, cols) for v in (send, keep))
    both = jnp.stack([jnp.where(core == 0, keep, send), jnp.where(core == 0, send, keep)], axis=1).astype(F32)
    if folds == 1:
        return both.reshape(GROUP * rows, cols)
    tiles = 4
    both = both.reshape(GROUP, 2, rows // 2, tiles, cols // tiles)
    return both.transpose(0, 2, 3, 1, 4).reshape(GROUP * rows // 2, 2 * cols)


def swap(value, axis, bit, size):
    return lax.ppermute(value, axis, [(i, i ^ bit) for i in range(size)])


def shards(img_size, args):
    (patches, grid_shape, split_rows, owner_shard, drop_masks, ln1_gain, ln1_bias, qkv_weight, qv_bias, proj_weight,
     proj_bias, ln2_gain, ln2_bias, fc1_weight, fc1_bias, fc2_weight, fc2_bias, cotangent) = args
    all_images, _, half, width = patches.shape
    images = all_images // 2
    rows = 2 * half
    tokens = images * rows
    side = lax.axis_index("seq")
    line = lax.axis_index("img")
    owners = 2 * img_size
    row = lambda v: v.reshape(1, -1)
    w = dict(
        ln1_gain=row(ln1_gain), ln1_bias=row(ln1_bias), qkv_weight=qkv_weight, q_bias=row(qv_bias[:width]),
        v_bias=row(qv_bias[width:]), proj_weight=proj_weight, proj_bias=row(proj_bias), ln2_gain=row(ln2_gain),
        ln2_bias=row(ln2_bias), fc1_weight=fc1_weight, fc1_bias=row(fc1_bias), fc2_weight=fc2_weight, fc2_bias=row(fc2_bias),
    )

    def exchange(value):
        value = value.reshape(all_images, half, width)
        own = lax.dynamic_slice_in_dim(value, side * images, images, axis=0)
        away = lax.dynamic_slice_in_dim(value, (1 - side) * images, images, axis=0)
        return own, swap(away, "seq", 1, 2)

    def restore(own, oth):
        back = swap(oth, "seq", 1, 2).astype(own.dtype)
        first = jnp.where(side == 0, own, back)
        second = jnp.where(side == 0, back, own)
        return jnp.concatenate([first, second], axis=0).reshape(all_images, 1, half, width)

    x_own, x_oth = exchange(patches)
    c_own, c_oth = exchange(cotangent)
    across = grid_shape[:, 1]
    counts = jnp.stack([split_rows * across, (grid_shape[:, 0] - split_rows) * across], axis=0)
    count_own = jnp.where(side == 0, counts[0], counts[1])
    count_oth = jnp.where(side == 0, counts[1], counts[0])
    special = (owner_shard == side).astype(jnp.int32)
    table = jnp.stack([count_own, special, count_oth, 1 - special, drop_masks[:, 0], drop_masks[:, 1]], axis=1)
    scal = lax.dynamic_slice_in_dim(table, side * images, images, axis=0)

    n1, qkv, probs, attended, middle, n2 = front(scal, x_own, x_oth, w)
    flat = lambda v: v.reshape(tokens, v.shape[-1])
    hidden, slope, out_own, out_oth = mlp(scal, flat(n2), flat(middle), w, images, 512)
    layer_out = restore(out_own, out_oth)

    mine = lax.rem(line, 2).reshape(1)
    unit1 = width // GROUP
    unit2 = fc2_weight.shape[0] // GROUP
    dn2, s2, k2, s1, k1, fc2_bias_grad, fc1_bias_grad = mlp_back(
        scal, mine, c_own, c_oth, flat(n2), hidden, slope, w, unit1, unit2
    )
    d_middle, d_branch, d_join, ln2_gain_grad, ln2_bias_grad, proj_bias_grad, q_grad, v_grad = attend_back(
        scal, c_own, c_oth, dn2.reshape(images, rows, width), middle, qkv, probs, w
    )
    st, kt, grad_own, grad_oth, ln1_gain_grad, ln1_bias_grad = tail(
        mine, flat(n1), flat(d_join), flat(attended), flat(d_branch), x_own, x_oth, flat(d_middle), w, unit1
    )
    patches_grad = restore(grad_own, grad_oth)
    vectors = (
        ln1_gain_grad, ln1_bias_grad, jnp.concatenate([q_grad, v_grad], axis=1), proj_bias_grad, ln2_gain_grad,
        ln2_bias_grad, fc1_bias_grad, fc2_bias_grad,
    )
    if owners == GROUP:
        small = jnp.concatenate([v.reshape(owners, -1) for v in vectors], axis=1)
        small = jnp.pad(small, ((0, 0), (0, 1024 - small.shape[1]))).reshape(owners, 8, 128)
        fc2_grad, fc1_grad, qkv_grad, proj_grad, small = reduce_all(s2, k2, s1, k1, st, kt, small)
        small = small.reshape(-1)
        pieces = []
        at = 0
        for v in vectors:
            pieces.append(small[at : at + v.shape[1] // owners])
            at += v.shape[1] // owners
    else:
        fc2_grad = spread(unfold(s2, k2, line % 2, 1))
        fc1_grad = spread(unfold(s1, k1, line % 2, 2))
        tail_grad = spread(unfold(st, kt, line % 2, 2))
        qkv_grad, proj_grad = tail_grad[:, : 3 * width], tail_grad[:, 3 * width :]
        pieces = [spread(v.reshape(-1)) for v in vectors]
    l1g, l1b, qvb, pjb, l2g, l2b, f1b, f2b = pieces
    return (
        layer_out, patches_grad, l1g, l1b, qkv_grad, qvb, proj_grad, pjb, l2g, l2b, fc1_grad, f1b, fc2_grad, f2b,
    )


def solution(mesh):
    rep = [P()] * 12
    vec = P(("img", "seq"))
    mat = P(("img", "seq"), None)
    rows = P("img", "seq", None, None)

    def run(*args):
        return shards(mesh.shape["img"], args)

    return jax.shard_map(
        run,
        mesh=mesh,
        in_specs=(rows, P("img", None), P("img"), P("img"), P("img", None), *rep, rows),
        out_specs=(rows, rows, vec, vec, mat, vec, mat, vec, vec, vec, mat, vec, mat, vec),
        check_vma=False,
    )
```

profile of v0, /device:TPU:0, one launch (start us, length us, event | category | flops | bytes accessed | tf_op | source)
XLA Modules:
  0.0 263.4 jit_solution(17924775810239397391)
XLA Ops:
  0.7 2.4 dynamic-slice_bitcast_fusion.2
  3.2 3.0 %collective-permute-start = (bf16[3,160,768]{2,1,0:T(8,128)(2,1)S(1)}, bf16[3,160,768]{2,1,0:T(8,128)(2,1)S(1)}, u32[]{:S(2)}, u32[]{:S(2)}) collective-permute-start(bf16[3,160,768]{2,1,0:T(8,128)(2,1)S(1)} %get-tuple-element.120), channel_id=1, source_target_pairs={{0,1},{1,0},{2,3},{3,2},{4,5},{5,4},{6,7},{7,6},{8,9},{9,8},{10,11... | collective-permute-start | bytes 2211848 | tf_op jit(solution)/shard_map/ppermute | solution.py:668
  6.2 1.0 dynamic-slice_bitcast_fusion
  7.2 0.1 copy.39
  7.3 0.1 copy.40
  7.4 0.1 copy.41
  7.5 0.1 copy.42
  7.6 0.1 copy.43
  7.7 0.6 reshape.134.g1_ref
  8.3 0.6 reshape.135.b1_ref
  8.9 0.6 reshape.136.qb_ref
  9.5 0.6 reshape.137.vb_ref
  10.0 0.6 reshape.138.pb_ref
  10.6 0.6 reshape.139.g2_ref
  11.2 0.6 reshape.140.b2_ref
  11.8 0.6 reshape.144.c2_ref
  12.5 0.6 constant_dynamic-slice_fusion.scal_ref
  13.1 10.4 %collective-permute-done.oth_ref.xt_ref = bf16[3,160,768]{2,1,0:T(8,128)(2,1)S(1)} collective-permute-done((bf16[3,160,768]{2,1,0:T(8,128)(2,1)S(1)}, bf16[3,160,768]{2,1,0:T(8,128)(2,1)S(1)}, u32[]{:S(2)}, u32[]{:S(2)}) %collective-permute-start) | collective-permute-done | bytes 737312 | tf_op jit(solution)/shard_map/ppermute | solution.py:668
  23.5 0.9 copy-done.23
  24.4 23.8 %front.1 = (bf16[3,320,768]{2,1,0:T(8,128)(2,1)}, bf16[3,320,2304]{2,1,0:T(8,128)(2,1)}, bf16[3,12,320,320]{3,2,1,0:T(8,128)(2,1)}, bf16[3,320,768]{2,1,0:T(8,12...) custom-call(s32[3,6]{1,0:T(4,128)} %constant_dynamic-slice_fusion.scal_ref, ...), custom_call_target="tpu_custom_call" | custom-call | flops 6417285120 | bytes 30000000 | tf_op jit(solution)/shard_map/front/pallas_call | solution.py:120
  48.2 25.6 %mlp.1 = (bf16[960,3072]{1,0:T(8,128)(2,1)}, bf16[960,3072]{1,0:T(8,128)(2,1)}, bf16[3,160,768]{2,1,0:T(8,128)(2,1)}, bf16[3,160,768]{2,1,0:T(8,128)(2,1)}) custom-call(s32[3,6]{1,0:T(4,128)} %constant_dynamic-slice_fusion.scal_ref, bf16[960,768]{1,0:T(8,128)(2,1)} %bitcast.78, f32[960,768]{1,0:T(8,128)} %bitcast.66, bf16[768,3072]{1,0:T(8,128)(2,1)} %w1_ref.3, ...), custom_call_target="tpu_custom_call" | custom-call | flops 9059696640 | bytes 30000000 | tf_op jit(solution)/shard_map/mlp/pallas_call | solution.py:186
  73.9 2.1 collective-permute-start.1
  76.0 0.9 copy-done.5
  76.9 30.4 %mlp_back.1 = (f32[960,768]{1,0:T(8,128)}, bf16[4,2,2,96,768]{4,3,2,1,0:T(8,128)(2,1)}, bf16[4,2,2,96,768]{4,3,2,1,0:T(8,128)(2,1)}, bf16[8,2,48,1536]{3,2,1,0:T...) custom-call(s32[3,6]{1,0:T(4,128)} %constant_dynamic-slice_fusion.scal_ref, ...), custom_call_target="tpu_custom_call" | custom-call | flops 18119393280 | bytes 35000000 | tf_op jit(solution)/shard_map/mlp_back/pallas_call | solution.py:287
  107.2 25.2 %attend_back.1 = (f32[3,320,768]{2,1,0:T(8,128)}, bf16[3,320,768]{2,1,0:T(8,128)(2,1)}, bf16[3,320,2304]{2,1,0:T(8,128)(2,1)}, f32[1,768]{1,0:T(1,128)}, f32[1,7...) custom-call(s32[3,6]{1,0:T(4,128)} %constant_dynamic-slice_fusion.scal_ref, ...), custom_call_target="tpu_custom_call" | custom-call | flops 4907335680 | bytes 35000000 | tf_op jit(solution)/shard_map/attend_back/pallas_call | solution.py:385
  132.5 18.3 %tail.1 = (bf16[8,2,48,1536]{3,2,1,0:T(8,128)(2,1)}, bf16[8,2,48,1536]{3,2,1,0:T(8,128)(2,1)}, f32[3,160,768]{2,1,0:T(8,128)}, bf16[3,160,768]{2,1,0:T(8,128)(2,1)}, f32[1,768]{1,0:T(1,128)}, /*index=5*/f32[1,768]{1,0:T(1,128)}) custom-call(s32[1]{0:T(128)} %bitcast.13.mine_ref, bf16[960,768]{1,0:T(8,128)(2,1)} %bitcast.76, bf16[960,2304]{1,0:T(8,128)(2,1)} %bitcast.72, ...), custom_call_target="tpu_custom_call" | custom-call | flops 7927234560 | bytes 35000000 | tf_op jit(solution)/shard_map/tail/pallas_call | solution.py:456
  150.9 0.7 reduce.1
  151.6 0.7 reduce.2
  152.5 0.1 reshape.161
  152.7 0.1 reshape.162
  152.9 0.5 broadcast.18
  153.4 0.7 reduce.12
  154.2 0.1 reshape.165
  154.2 0.1 concatenate.15
  154.4 1.7 copy-done.1
  156.1 97.6 %reduce.13 = (f32[96,768]{1,0:T(8,128)S(1)}, f32[24,3072]{1,0:T(8,128)S(1)}, f32[24,2304]{1,0:T(8,128)S(1)}, f32[24,768]{1,0:T(8,128)S(1)}, f32[8,128]{1,0:T(8,128)S(1)}) custom-call(bf16[4,2,2,96,768]{4,3,2,1,0:T(8,128)(2,1)S(1)} %copy-done, bf16[4,2,2,96,768]{4,3,2,1,0:T(8,128)(2,1)S(1)} %copy-done.1, bf16[4,2,2,48,1536]{4,3,2,1,0:T(8,128)(2,1)} %bitcast.68, ...), custom_call_target="tpu_custom_call" | custom-call | tf_op jit(solution)/shard_map/reduce/pallas_call | solution.py:621
  253.7 0.6 slice.45
  254.3 0.6 slice.49
  254.9 0.6 fusion.5
  255.5 0.1 broadcast_select_fusion.1
  255.6 1.2 maximum_bitcast_fusion.1
  256.8 0.7 copy-done.3
  257.5 1.4 convert_select_fusion.1
  258.9 1.8 maximum_bitcast_fusion
  260.7 0.7 copy.51
  261.4 0.6 copy.52
  262.0 0.7 copy.53
  262.7 0.7 copy.54
  (68 shorter events, 0.8 us)
Async XLA Ops:
  0.7 5.5 %copy-start.2 = (bf16[6,1,160,768]{3,2,1,0:T(8,128)(2,1)S(1)}, bf16[6,1,160,768]{3,2,1,0:T(8,128)(2,1)}, u32[]{:S(2)}) copy-start(bf16[6,1,160,768]{3,2,1,0:T(8,128)(2,1)} %param.35) | copy-start | bytes 4423684
  3.1 4.1 %copy-start.20 = (s32[6,2]{0,1:T(2,128)S(1)}, s32[6,2]{0,1:T(2,128)}, u32[]{:S(2)}) copy-start(s32[6,2]{0,1:T(2,128)} %param.19) | copy-start | bytes 148
  3.1 4.1 %copy-start.22 = (s32[6]{0:T(128)S(1)}, s32[6]{0:T(128)}, u32[]{:S(2)}) copy-start(s32[6]{0:T(128)} %param.20) | copy-start | bytes 76
  3.1 4.2 %copy-start.24 = (s32[6]{0:T(128)S(1)}, s32[6]{0:T(128)}, u32[]{:S(2)}) copy-start(s32[6]{0:T(128)} %param.21) | copy-start | bytes 76
  3.1 4.5 %copy-start.21 = (s32[6,2]{0,1:T(2,128)S(1)}, s32[6,2]{0,1:T(2,128)}, u32[]{:S(2)}) copy-start(s32[6,2]{0,1:T(2,128)} %param.22) | copy-start | bytes 148
  3.1 4.6 %copy-start.8 = (f32[768]{0:T(1024)S(1)}, f32[768]{0:T(1024)}, u32[]{:S(2)}) copy-start(f32[768]{0:T(1024)} %param.23) | copy-start | bytes 9220
  3.1 5.2 %copy-start.9 = (f32[768]{0:T(1024)S(1)}, f32[768]{0:T(1024)}, u32[]{:S(2)}) copy-start(f32[768]{0:T(1024)} %param.24) | copy-start | bytes 9220
  3.1 5.8 %copy-start.7 = (f32[1536]{0:T(1024)S(1)}, f32[1536]{0:T(1024)}, u32[]{:S(2)}) copy-start(f32[1536]{0:T(1024)} %param.26) | copy-start | bytes 18436
  3.1 6.9 %copy-start.10 = (f32[768]{0:T(1024)S(1)}, f32[768]{0:T(1024)}, u32[]{:S(2)}) copy-start(f32[768]{0:T(1024)} %param.28) | copy-start | bytes 9220
  3.1 7.5 %copy-start.11 = (f32[768]{0:T(1024)S(1)}, f32[768]{0:T(1024)}, u32[]{:S(2)}) copy-start(f32[768]{0:T(1024)} %param.29) | copy-start | bytes 9220
  3.1 8.1 %copy-start.12 = (f32[768]{0:T(1024)S(1)}, f32[768]{0:T(1024)}, u32[]{:S(2)}) copy-start(f32[768]{0:T(1024)} %param.30) | copy-start | bytes 9220
  3.2 8.7 %copy-start.13 = (f32[768]{0:T(1024)S(1)}, f32[768]{0:T(1024)}, u32[]{:S(2)}) copy-start(f32[768]{0:T(1024)} %param.34) | copy-start | bytes 9220
  3.2 20.3 %collective-permute-start = (bf16[3,160,768]{2,1,0:T(8,128)(2,1)S(1)}, bf16[3,160,768]{2,1,0:T(8,128)(2,1)S(1)}, u32[]{:S(2)}, u32[]{:S(2)}) collective-permute-start(bf16[3,160,768]{2,1,0:T(8,128)(2,1)S(1)} %get-tuple-element.120), channel_id=1, source_target_pairs={{0,1},{1,0},{2,3},{3,2},{4,5},{5,4},{6,7},{7,6},{8,9},{9,8},{10,11... | collective-permute-start | bytes 2211848 | tf_op jit(solution)/shard_map/ppermute | solution.py:668
  7.2 68.8 %collective-permute-start.2 = (bf16[3,160,768]{2,1,0:T(8,128)(2,1)S(1)}, bf16[3,160,768]{2,1,0:T(8,128)(2,1)S(1)}, u32[]{:S(2)}, u32[]{:S(2)}) collective-permute-start(bf16[3,160,768]{2,1,0:T(8,128)(2,1)S(1)} %get-tuple-element.116), channel_id=1, source_target_pairs={{0,1},{1,0},{2,3},{3,2},{4,5},{5,4},{6,7},{7,6},{8,9},{9,8},{10,11... | collective-permute-start | bytes 2211848 | tf_op jit(solution)/shard_map/ppermute | solution.py:668
  23.5 0.9 copy-start.23
  73.9 181.6 %collective-permute-start.1 = (bf16[3,160,768]{2,1,0:T(8,128)(2,1)}, bf16[3,160,768]{2,1,0:T(8,128)(2,1)S(1)}, u32[]{:S(2)}, u32[]{:S(2)}) collective-permute-start(bf16[3,160,768]{2,1,0:T(8,128)(2,1)} %get-tuple-element.53), channel_id=1, source_target_pairs={{0,1},{1,0},{2,3},{3,2},{4,5},{5,4},{6,7},{7,6},{8,9},{9,8},{10,11... | collective-permute-start | bytes 2211848 | tf_op jit(solution)/shard_map/ppermute | solution.py:668
  76.0 0.9 copy-start.5
  132.4 20.0 %copy-start.14 = (f32[1,768]{1,0:T(1,128)S(1)}, f32[1,768]{1,0:T(1,128)}, u32[]{:S(2)}) copy-start(f32[1,768]{1,0:T(1,128)} %get-tuple-element.74) | copy-start | bytes 9220
  132.4 20.0 %copy-start.15 = (f32[1,768]{1,0:T(1,128)S(1)}, f32[1,768]{1,0:T(1,128)}, u32[]{:S(2)}) copy-start(f32[1,768]{1,0:T(1,128)} %get-tuple-element.75) | copy-start | bytes 9220
  132.5 20.1 %copy-start.19 = (f32[1,768]{1,0:T(1,128)S(1)}, f32[1,768]{1,0:T(1,128)}, u32[]{:S(2)}) copy-start(f32[1,768]{1,0:T(1,128)} %get-tuple-element.76) | copy-start | bytes 9220
  132.5 20.2 %copy-start.18 = (f32[1,768]{1,0:T(1,128)S(1)}, f32[1,768]{1,0:T(1,128)}, u32[]{:S(2)}) copy-start(f32[1,768]{1,0:T(1,128)} %get-tuple-element.77) | copy-start | bytes 9220
  132.5 20.3 %copy-start.17 = (f32[1,768]{1,0:T(1,128)S(1)}, f32[1,768]{1,0:T(1,128)}, u32[]{:S(2)}) copy-start(f32[1,768]{1,0:T(1,128)} %get-tuple-element.78) | copy-start | bytes 9220
  132.5 20.9 %copy-start.6 = (f32[1,3072]{1,0:T(1,128)S(1)}, f32[1,3072]{1,0:T(1,128)}, u32[]{:S(2)}) copy-start(f32[1,3072]{1,0:T(1,128)} %get-tuple-element.79) | copy-start | bytes 36868
  132.5 21.6 %copy-start.16 = (f32[1,768]{1,0:T(1,128)S(1)}, f32[1,768]{1,0:T(1,128)}, u32[]{:S(2)}) copy-start(f32[1,768]{1,0:T(1,128)} %get-tuple-element.80) | copy-start | bytes 9220
  132.5 21.9 %copy-start = (bf16[4,2,2,96,768]{4,3,2,1,0:T(8,128)(2,1)S(1)}, bf16[4,2,2,96,768]{4,3,2,1,0:T(8,128)(2,1)}, u32[]{:S(2)}) copy-start(bf16[4,2,2,96,768]{4,3,2,1,0:T(8,128)(2,1)} %get-tuple-element.66.s2_ref) | copy-start | bytes 7077892
  150.8 106.1 %collective-permute-start.3 = (bf16[3,160,768]{2,1,0:T(8,128)(2,1)}, bf16[3,160,768]{2,1,0:T(8,128)(2,1)}, u32[]{:S(2)}, u32[]{:S(2)}) collective-permute-start(bf16[3,160,768]{2,1,0:T(8,128)(2,1)} %get-tuple-element.65), channel_id=1, source_target_pairs={{0,1},{1,0},{2,3},{3,2},{4,5},{5,4},{6,7},{7,6},{8,9},{9,8},{10,11... | collective-permute-start | bytes 2211848 | tf_op jit(solution)/shard_map/ppermute | solution.py:668
  154.4 1.7 copy-start.1
  156.1 99.4 %copy-start.4 = (bf16[3,160,768]{2,1,0:T(8,128)(2,1)S(1)}, bf16[3,160,768]{2,1,0:T(8,128)(2,1)}, u32[]{:S(2)}) copy-start(bf16[3,160,768]{2,1,0:T(8,128)(2,1)} %get-tuple-element.52) | copy-start | bytes 2211844
  255.6 1.9 copy-start.3
where the time goes:
time: 264 us; the launch traced here: 263 us
  Pallas kernels  221 us (84%)
  local copies, waits for them, and re-layouts  19.2 us (7%)
  waiting for transfers between devices  10.4 us (4%)
  other arithmetic  6.66 us (3%)
  starting transfers between devices  5.23 us (2%)
    pallas_call x1, Pallas kernels, reduce_all(): pl.pallas_call(reduce_kernel, in_specs=[hbm] * 6 + [vmem], out_specs=[vme...  97.6 us
    pallas_call x1, Pallas kernels, mlp_back(): pl.pallas_call(mlp_back_kernel, grid_spec=pltpu.PrefetchScalarGridSpec(nu...  30.4 us
    pallas_call x1, Pallas kernels, mlp(): pl.pallas_call(mlp_kernel, grid_spec=pltpu.PrefetchScalarGridSpec(num_sca...  25.6 us
    pallas_call x1, Pallas kernels, attend_back(): pl.pallas_call(attend_back_kernel, grid_spec=pltpu.PrefetchScalarGridSpec...  25.2 us
    pallas_call x1, Pallas kernels, front(): pl.pallas_call(front_kernel, grid_spec=pltpu.PrefetchScalarGridSpec(num_s...  23.8 us
    pallas_call x1, Pallas kernels, tail(): pl.pallas_call(tail_kernel, grid_spec=pltpu.PrefetchScalarGridSpec(num_sc...  18.3 us
    ppermute x4, waiting for transfers between devices, swap(): return lax.ppermute(value, axis, [(i, i ^ bit) for i in range(size)])  10.4 us
    unnamed x57, local copies, waits for them, and re-layouts  7.07 us
  transfers between devices with their start and end apart: 4, of which 1 were waited for; matrix products, arithmetic and copies ran while one was open for 5% of the time, Pallas kernels for 84%

commit v1 on v0

--- a/solution.py
+++ b/solution.py
@@ -486,14 +486,37 @@
 MESH = pl.DeviceIdType.MESH
 DEPTH, LEVELS = 4, 2
 PARTS = 6
+SLOTS = 3
 GROUP = 32
 
 
-def reduce_kernel(
-    s2_ref, k2_ref, s1_ref, k1_ref, st_ref, kt_ref, small_ref,
-    fc2_ref, fc1_ref, qkv_ref, proj_ref, tiny_ref,
-    keep_ref, rc_ref, ra_ref, rb_ref, rz_ref, keep_t, rc_t, ra_t, rb_t, rz_t, load_sem, send_sem, recv_sem,
+class Far:
+    def __init__(self, ends, send_sem, recv_sem, peer):
+        self.parts = (ends, send_sem, recv_sem, peer)
+        self.build().start()
+
+    def build(self):
+        ends, send_sem, recv_sem, peer = self.parts
+        src, dst = ends()
+        return pltpu.make_async_remote_copy(
+            src_ref=src, dst_ref=dst, send_sem=send_sem(), recv_sem=recv_sem(), device_id=peer, device_id_type=MESH
+        )
+
+    def wait(self):
+        self.build().wait()
+
+
+def finish_kernel(
+    scal_ref, cot_own, cot_oth, dn2_hbm, mid_hbm, qkv_hbm, probs_hbm, wp_hbm, wqkv_hbm, n1_hbm, att_hbm, x_own, x_oth,
+    s2_ref, k2_ref, s1_ref, k1_ref, g1_ref, g2_ref, c1_ref, c2_ref,
+    fc2_ref, fc1_ref, qkvg_ref, projg_ref, vec_ref, grad_ref, back_ref,
+    cot, xin, dn2, mid, qkv, probs, wp, wqkv, n1, att, dbr, djoin, datt, tile, gout, gsend, grecv, vec, vget,
+    keep, send, rc, ra, rb, rz,
+    load_sem, probs_sem, send_sem, recv_sem, side_send, side_recv, vec_send, vec_recv, out_sem, free_sem,
 ):
+    images, rows, width = dn2.shape
+    half = rows // 2
+    pairs = width // 128
     line = lax.axis_index("img")
     x = lax.axis_index("seq")
     core = line % 2
@@ -507,146 +530,333 @@
     barrier = pltpu.get_barrier_semaphore()
     for peer in peers:
         pl.semaphore_signal(barrier, inc=1, device_id=peer, device_id_type=MESH)
+
+    loads = []
+
+    def fetch(src, dst):
+        copy = pltpu.make_async_copy(src, dst, load_sem.at[len(loads)])
+        copy.start()
+        loads.append(copy)
+        return copy
+
+    def probs_copy(index, slot):
+        return pltpu.make_async_copy(
+            probs_hbm.at[index // pairs, pl.ds(2 * (index % pairs), 2)], probs.at[slot], probs_sem.at[slot]
+        )
+
+    first = [fetch(cot_own, cot.at[:, pl.ds(0, half)]), fetch(cot_oth, cot.at[:, pl.ds(half, half)])]
+    first += [fetch(mid_hbm, mid), fetch(dn2_hbm, dn2), fetch(wp_hbm, wp), fetch(qkv_hbm, qkv)]
+    for slot in range(SLOTS):
+        probs_copy(slot, slot).start()
+    r, c = keep.shape[-2], keep.shape[-1]
+    keep_src = [k2_ref.at[:, :, :, pl.ds(k * r, r), :] for k in range(2)]
+    keep_src += [k1_ref.at[:, :, :, :, pl.ds(k * c, c)] for k in range(2)]
+    send_src = [s2_ref.at[:, :, :, pl.ds(k * r, r), :] for k in range(2)]
+    send_src += [s1_ref.at[:, :, :, :, pl.ds(k * c, c)] for k in range(2)]
+    keep_in = [fetch(keep_src[k], keep.at[k]) for k in range(4)]
+    late = [fetch(n1_hbm, n1), fetch(att_hbm, att), fetch(wqkv_hbm, wqkv)]
+    late += [fetch(x_own, xin.at[:, pl.ds(0, half)]), fetch(x_oth, xin.at[:, pl.ds(half, half)])]
     pl.semaphore_wait(barrier, len(peers))
 
-    rows, cols = keep_ref.shape[-2], keep_ref.shape[-1]
-    pick = []
-    for k in range(2):
-        pick.append((s2_ref.at[:, :, :, pl.ds(k * rows, rows), :], k2_ref.at[:, :, :, pl.ds(k * rows, rows), :]))
-    for s_ref, k_ref in ((s1_ref, k1_ref), (st_ref, kt_ref)):
-        for k in range(2):
-            pick.append((s_ref.at[:, :, :, :, pl.ds(k * cols, cols)], k_ref.at[:, :, :, :, pl.ds(k * cols, cols)]))
-
-    def far(src, dst, part, slot, peer):
-        copy = pltpu.make_async_remote_copy(
-            src_ref=src, dst_ref=dst, send_sem=send_sem.at[part, slot], recv_sem=recv_sem.at[part, slot],
-            device_id=peer, device_id_type=MESH,
-        )
-        copy.start()
-        return copy
+    def far(ends, part, slot, peer):
+        return Far(ends, lambda: send_sem.at[part, slot], lambda: recv_sem.at[part, slot], peer)
 
     pending = {}
-    loads = []
-    for part, (send, keep) in enumerate(pick):
-        pending[part] = far(send, rc_ref.at[part], part, 0, sibling)
-        load = pltpu.make_async_copy(keep, keep_ref.at[part], load_sem.at[part])
-        load.start()
-        loads.append(load)
-    keep_t[...] = small_ref[:, :, pl.ds(core, 1)].reshape(keep_t.shape)
-    pending[PARTS] = far(small_ref.at[:, :, 1 - core], rc_t, PARTS, 0, sibling)
+    rc_slot = [0, 1, 2, 3, 0, 1]
+    for part in range(4):
+        pending[part] = far(lambda part=part: (send_src[part], rc.at[part]), part, 0, sibling)
 
     def add(target, source):
         target[...] = (target[...].astype(F32) + source[...].astype(F32)).astype(target.dtype)
 
-    def stage_one(part, kept, rc, ra, first_level):
+    def stage_one(part):
         pending[part].wait()
-        if part < PARTS:
-            loads[part].wait()
+        if part < 4:
+            keep_in[part].wait()
+        first_level = part % 2 == 0
+        kept, arrived = keep.at[part], rc.at[rc_slot[part]]
 
         @pl.loop(0, DEPTH * 2)
         def _(i):
-            a, b = i // 2, i % 2
-            for c in range(2):
-                add(kept.at[a, b, c], rc.at[a, b, c])
-
-        src = kept.at[:, 1 - y] if first_level else kept.at[:, :, 1 - x]
-        pending[part] = far(src, ra, part, 1, level if first_level else across)
-
-    def stage_two(part, kept, ra, rb, first_level):
+            p, q = i // 2, i % 2
+            for e in range(2):
+                add(kept.at[p, q, e], arrived.at[p, q, e])
+
+        if part < 2:
+            pl.semaphore_signal(free_sem.at[part], inc=1, device_id=sibling, device_id_type=MESH)
+        def ends():
+            src = keep.at[part, :, 1 - y] if first_level else keep.at[part, :, :, 1 - x]
+            return src, ra.at[part]
+
+        pending[part] = far(ends, part, 1, level if first_level else across)
+
+    def stage_two(part):
         pending[part].wait()
+        first_level = part % 2 == 0
+        kept, arrived = keep.at[part], ra.at[part]
 
         @pl.loop(0, DEPTH * 2)
         def _(i):
-            a, b = i // 2, i % 2
-            add(kept.at[a, y, b] if first_level else kept.at[a, b, x], ra.at[a, b])
-
-        src = kept.at[:, y, 1 - x] if first_level else kept.at[:, 1 - y, x]
-        pending[part] = far(src, rb, part, 2, across if first_level else level)
-
-    def stage_three(part, kept, rb, rz):
+            p, q = i // 2, i % 2
+            add(kept.at[p, y, q] if first_level else kept.at[p, q, x], arrived.at[p, q])
+
+        def ends():
+            src = keep.at[part, :, y, 1 - x] if first_level else keep.at[part, :, 1 - y, x]
+            return src, rb.at[part]
+
+        pending[part] = far(ends, part, 2, across if first_level else level)
+
+    def stage_three(part):
         pending[part].wait()
+        kept, arrived = keep.at[part], rb.at[part]
 
         @pl.loop(0, DEPTH)
-        def _(a):
-            add(kept.at[a, y, x], rb.at[a])
+        def _(p):
+            add(kept.at[p, y, x], arrived.at[p])
 
         pending[part] = [
-            far(kept.at[(z + d) % DEPTH, y, x], rz.at[d - 1], part, 2 + d, deep[d - 1]) for d in range(1, DEPTH)
+            far(lambda d=d: (keep.at[part, (z + d) % DEPTH, y, x], rz.at[part, d - 1]), part, 2 + d, deep[d - 1])
+            for d in range(1, DEPTH)
         ]
 
-    def stage_four(part, kept, rz):
+    def stage_four(part):
         for copy in pending[part]:
             copy.wait()
-        total = kept[z, y, x].astype(F32)
+        total = keep[part, z, y, x].astype(F32)
         for d in range(DEPTH - 1):
-            total += rz[d].astype(F32)
-        return total
-
-    for part in range(PARTS):
-        stage_one(part, keep_ref.at[part], rc_ref.at[part], ra_ref.at[part], part % 2 == 0)
-    stage_one(PARTS, keep_t, rc_t, ra_t, True)
-    for part in range(PARTS):
-        stage_two(part, keep_ref.at[part], ra_ref.at[part], rb_ref.at[part], part % 2 == 0)
-    stage_two(PARTS, keep_t, ra_t, rb_t, True)
-    for part in range(PARTS):
-        stage_three(part, keep_ref.at[part], rb_ref.at[part], rz_ref.at[part])
-    stage_three(PARTS, keep_t, rb_t, rz_t)
-    unit, side = rows // 2, cols // 2
-    for part in range(PARTS):
-        total = stage_four(part, keep_ref.at[part], rz_ref.at[part])
+            total += rz[part, d].astype(F32)
+        unit, side = r // 2, c // 2
         if part < 2:
-            fc2_ref[part * rows : part * rows + rows, :] = total
-            continue
+            fc2_ref[part * r : part * r + r, :] = total
+            return
         for t in range(2):
             for h in range(2):
                 piece = total[h * unit : h * unit + unit, t * side : t * side + side]
-                at = ((part % 2) * 2 + t) * cols + h * side
+                at = ((part % 2) * 2 + t) * c + h * side
                 if part < 4:
                     fc1_ref[:, at : at + side] = piece
-                elif at < 3 * cols:
-                    qkv_ref[:, at : at + side] = piece
+                elif at < 3 * c:
+                    qkvg_ref[:, at : at + side] = piece
                 else:
-                    proj_ref[:, at - 3 * cols : at - 3 * cols + side] = piece
-    tiny_ref[...] = stage_four(PARTS, keep_t, rz_t)
-
-
-def reduce_all(s2, k2, s1, k1, st, kt, small):
-    rows, cols = s1.shape[-2], s1.shape[-1] // 2
-    unit = rows // 2
-    s2, k2 = s2.reshape(DEPTH, 2, 2, 2 * rows, cols), k2.reshape(DEPTH, 2, 2, 2 * rows, cols)
-    s1, k1, st, kt = (v.reshape(DEPTH, 2, 2, rows, 2 * cols) for v in (s1, k1, st, kt))
-    small = small.reshape(DEPTH, 2, 2, 2, 8, 128)
+                    projg_ref[:, at - 3 * c : at - 3 * c + side] = piece
+
+    vec[...] = jnp.zeros_like(vec)
+    for k in range(4):
+        vec[7 + k : 8 + k, :] = c1_ref[:, k * width : k * width + width]
+    vec[11:12, :] = c2_ref[...]
+    for copy in first:
+        copy.wait()
+    low_lane = lax.broadcasted_iota(jnp.int32, (rows, 128), 1) < HEAD_DIM
+    plan = {
+        (0, 0): [(stage_one, 0)], (0, 1): [(stage_one, 1)], (0, 2): [(stage_one, 2)], (0, 3): [(stage_one, 3)],
+        (2, 0): [(stage_two, 0)], (2, 1): [(stage_two, 1)],
+    }
+    def image_body(i):
+        live = row_valid(scal_ref, i, rows, half, 0)
+        d_final = jnp.where(live, cot[i].astype(F32), 0.0)
+        unit, rstd = norm_parts(mid[i])
+        d_normed = dn2[i]
+        vec[5:6, :] += jnp.sum(d_normed * unit, axis=0, keepdims=True)
+        vec[6:7, :] += jnp.sum(d_normed, axis=0, keepdims=True)
+        d_middle = d_final + norm_back(d_normed, g2_ref[...], unit, rstd)
+        dn2[i] = d_middle
+        gate = scal_ref[i, 4].astype(F32) * KEEP_SCALE
+        d_branch = (d_middle * gate).astype(BF16)
+        dbr[i] = d_branch
+        vec[4:5, :] += jnp.sum(d_branch.astype(F32), axis=0, keepdims=True)
+        datt[...] = dot_nt(d_branch, wp[...]).astype(BF16)
+        for pair in range(pairs):
+            index = i * pairs + pair
+            slot = index % SLOTS
+            probs_copy(index, slot).wait()
+            cut = slice(128 * pair, 128 * pair + 128)
+            k_cut = slice(width + 128 * pair, width + 128 * pair + 128)
+            v_cut = slice(2 * width + 128 * pair, 2 * width + 128 * pair + 128)
+            q2, k2, v2, a2 = qkv[i, :, cut], qkv[i, :, k_cut], qkv[i, :, v_cut], datt[:, cut]
+            dq = dk = dv = None
+            for side in range(2):
+                mine = low_lane if side == 0 else jnp.logical_not(low_lane)
+                low = probs[slot, side]
+                high = low.astype(F32)
+                a_side = jnp.where(mine, a2, 0)
+                d_probs = dot_nt(a_side, v2)
+                inner = jnp.sum(high * d_probs, axis=-1, keepdims=True)
+                d_scores = (high * (d_probs - inner)).astype(BF16)
+                parts = (dot_nn(d_scores, jnp.where(mine, k2, 0)), dot_tn(d_scores, jnp.where(mine, q2, 0)), dot_tn(low, a_side))
+                dq, dk, dv = parts if dq is None else (dq + parts[0], dk + parts[1], dv + parts[2])
+            djoin[i, :, cut] = (dq * HEAD_DIM**-0.5).astype(BF16)
+            djoin[i, :, k_cut] = dk.astype(BF16)
+            djoin[i, :, v_cut] = dv.astype(BF16)
+
+            @pl.when(index + SLOTS < images * pairs)
+            def _():
+                probs_copy(index + SLOTS, slot).start()
+
+            yield pair
+        vec[2:3, :] += jnp.sum(djoin[i, :, :width].astype(F32), axis=0, keepdims=True)
+        vec[3:4, :] += jnp.sum(djoin[i, :, 2 * width :].astype(F32), axis=0, keepdims=True)
+
+    @pl.loop(0, images)
+    def _(i):
+        for pair in image_body(i):
+            for (image, at), jobs in plan.items():
+                if at != pair:
+                    continue
+
+                @pl.when(i == image)
+                def _():
+                    for job, part in jobs:
+                        job(part)
+
+    for copy in late:
+        copy.wait()
+    flat = lambda ref: ref[...].reshape(images * rows, ref.shape[-1])
+
+    def weight_tile(t):
+        if t < 3:
+            value = dot_tn(flat(n1), djoin[:, :, t * width : t * width + width].reshape(images * rows, width))
+        else:
+            value = dot_tn(flat(att), flat(dbr))
+        tile[...] = value
+        part = 4 + t // 2
+        unit, side = r // 2, c // 2
+        spot = slice((t % 2) * side, (t % 2) * side + side)
+        for k in range(DEPTH * 2):
+            for ref, who in ((send.at[part - 4], 1 - core), (keep.at[part], core)):
+                for e in range(2):
+                    at = pl.multiple_of((4 * k + 2 * who + e) * unit, 8)
+                    piece = tile[pl.ds(at, unit), :]
+                    folded = jnp.concatenate([piece[:, :side], piece[:, side:]], axis=0).astype(BF16)
+                    ref[k // 2, k % 2, e, :, spot] = folded
+
+    def start_part(part):
+        pl.semaphore_wait(free_sem.at[part - 4], 1)
+        pending[part] = far(lambda: (send.at[part - 4], rc.at[rc_slot[part]]), part, 0, sibling)
+
+    weight_tile(3)
+    weight_tile(2)
+    start_part(5)
+    stage_two(2)
+    weight_tile(0)
+    stage_three(0)
+    weight_tile(1)
+    start_part(4)
+    stage_two(3)
+    stage_three(1)
+
+    def input_grad(i):
+        unit, rstd = norm_parts(xin[i].astype(F32))
+        d_normed = dot_nt(djoin[i], wqkv[...])
+        vec[0:1, :] += jnp.sum(d_normed * unit, axis=0, keepdims=True)
+        vec[1:2, :] += jnp.sum(d_normed, axis=0, keepdims=True)
+        out = dn2[i] + norm_back(d_normed, g1_ref[...], unit, rstd)
+        gout[i] = out[:half]
+        gsend[i] = out[half:].astype(BF16)
+
+    moves = []
+    swaps = []
+    for i in range(images):
+        input_grad(i)
+        swaps.append(
+            Far(lambda i=i: (gsend.at[i], grecv.at[i]), lambda i=i: side_send.at[i], lambda i=i: side_recv.at[i], across)
+        )
+        if i == 0:
+            stage_one(5)
+        if i == 1:
+            stage_one(4)
+            stage_three(2)
+    local = pltpu.make_async_copy(gout, grad_ref, out_sem.at[0])
+    local.start()
+    stage_three(3)
+
+    def exchange(k, peer):
+        return Far(lambda: (vec, vget.at[k]), lambda: vec_send.at[k], lambda: vec_recv.at[k], peer)
+
+    for k, peer in enumerate((sibling, level, across)):
+        exchange(k, peer).wait()
+        vec[...] += vget[k]
+        if k == 0:
+            stage_two(5)
+        if k == 1:
+            stage_two(4)
+    rest = [exchange(2 + d, deep[d - 1]) for d in range(1, DEPTH)]
+    stage_four(0)
+    stage_four(1)
+    stage_three(5)
+    stage_three(4)
+    stage_four(2)
+    stage_four(3)
+    for copy in rest:
+        copy.wait()
+    vec_ref[...] = vec[...] + vget[3] + vget[4] + vget[5]
+    for copy in swaps:
+        copy.wait()
+    other = pltpu.make_async_copy(grecv, back_ref, out_sem.at[1])
+    other.start()
+    stage_four(5)
+    stage_four(4)
+    local.wait()
+    other.wait()
+
+
+def finish(scal, cot_own, cot_oth, dn2, middle, qkv, probs, n1, attended, x_own, x_oth, s2, k2, s1, k1, c1, c2, w):
+    images, half, width = cot_own.shape
+    rows = 2 * half
+    heads = width // HEAD_DIM
+    r, c = s1.shape[-2], s1.shape[-1] // 2
+    s2, k2 = (v.reshape(DEPTH, 2, 2, 2 * r, c) for v in (s2, k2))
+    s1, k1 = (v.reshape(DEPTH, 2, 2, r, 2 * c) for v in (s1, k1))
     hbm = pl.BlockSpec(memory_space=pl.ANY)
     vmem = pl.BlockSpec(memory_space=pltpu.VMEM)
+    smem = pl.BlockSpec(memory_space=pltpu.SMEM)
+    dma = pltpu.SemaphoreType.DMA
+    block = lambda dtype, *lead: pltpu.VMEM(lead + (r, c), dtype)
     return pl.pallas_call(
-        reduce_kernel,
-        in_specs=[hbm] * 6 + [vmem],
-        out_specs=[vmem] * 5,
+        finish_kernel,
+        in_specs=[smem] + [hbm] * 16 + [vmem] * 4,
+        out_specs=[vmem] * 5 + [hbm] * 2,
         out_shape=[
-            jax.ShapeDtypeStruct((2 * rows, cols), F32),
-            jax.ShapeDtypeStruct((unit, 4 * cols), F32),
-            jax.ShapeDtypeStruct((unit, 3 * cols), F32),
-            jax.ShapeDtypeStruct((unit, cols), F32),
-            jax.ShapeDtypeStruct((8, 128), F32),
+            jax.ShapeDtypeStruct((2 * r, c), F32),
+            jax.ShapeDtypeStruct((r // 2, 4 * c), F32),
+            jax.ShapeDtypeStruct((r // 2, 3 * c), F32),
+            jax.ShapeDtypeStruct((r // 2, c), F32),
+            jax.ShapeDtypeStruct((16, width), F32),
+            jax.ShapeDtypeStruct((images, half, width), F32),
+            jax.ShapeDtypeStruct((images, half, width), BF16),
         ],
         scratch_shapes=[
-            pltpu.VMEM((PARTS, DEPTH, 2, 2, rows, cols), BF16),
-            pltpu.VMEM((PARTS, DEPTH, 2, 2, rows, cols), BF16),
-            pltpu.VMEM((PARTS, DEPTH, 2, rows, cols), BF16),
-            pltpu.VMEM((PARTS, DEPTH, rows, cols), BF16),
-            pltpu.VMEM((PARTS, DEPTH - 1, rows, cols), BF16),
-            pltpu.VMEM((DEPTH, 2, 2, 8, 128), F32),
-            pltpu.VMEM((DEPTH, 2, 2, 8, 128), F32),
-            pltpu.VMEM((DEPTH, 2, 8, 128), F32),
-            pltpu.VMEM((DEPTH, 8, 128), F32),
-            pltpu.VMEM((DEPTH - 1, 8, 128), F32),
-            pltpu.SemaphoreType.DMA((PARTS,)),
-            pltpu.SemaphoreType.DMA((PARTS + 1, 6)),
-            pltpu.SemaphoreType.DMA((PARTS + 1, 6)),
+            pltpu.VMEM((images, rows, width), BF16),
+            pltpu.VMEM((images, rows, width), BF16),
+            pltpu.VMEM((images, rows, width), F32),
+            pltpu.VMEM((images, rows, width), F32),
+            pltpu.VMEM((images, rows, 3 * width), BF16),
+            pltpu.VMEM((SLOTS, 2, rows, rows), BF16),
+            pltpu.VMEM((width, width), BF16),
+            pltpu.VMEM((width, 3 * width), BF16),
+            pltpu.VMEM((images, rows, width), BF16),
+            pltpu.VMEM((images, rows, width), BF16),
+            pltpu.VMEM((images, rows, width), BF16),
+            pltpu.VMEM((images, rows, 3 * width), BF16),
+            pltpu.VMEM((rows, width), BF16),
+            pltpu.VMEM((width, width), F32),
+            pltpu.VMEM((images, half, width), F32),
+            pltpu.VMEM((images, half, width), BF16),
+            pltpu.VMEM((images, half, width), BF16),
+            pltpu.VMEM((16, width), F32),
+            pltpu.VMEM((6, 16, width), F32),
+            block(BF16, PARTS, DEPTH, 2, 2),
+            block(BF16, 2, DEPTH, 2, 2),
+            block(BF16, 4, DEPTH, 2, 2),
+            block(BF16, PARTS, DEPTH, 2),
+            block(BF16, PARTS, DEPTH),
+            block(BF16, PARTS, DEPTH - 1),
+            dma((16,)), dma((SLOTS,)), dma((PARTS, 6)), dma((PARTS, 6)), dma((images,)), dma((images,)),
+            dma((6,)), dma((6,)), dma((2,)), pltpu.SemaphoreType.REGULAR((2,)),
         ],
-        compiler_params=pltpu.CompilerParams(collective_id=0, has_side_effects=True, vmem_limit_bytes=48 * MIB),
-        name="reduce",
-    )(s2, k2, s1, k1, st, kt, small)
+        compiler_params=pltpu.CompilerParams(collective_id=0, has_side_effects=True, vmem_limit_bytes=63 * MIB),
+        name="finish",
+    )(scal, cot_own, cot_oth, dn2, middle, qkv, probs, w["proj_weight"], w["qkv_weight"], n1, attended, x_own, x_oth,
+      s2, k2, s1, k1, w["ln1_gain"], w["ln2_gain"], c1, c2)
 
 
 def spread(value):
@@ -691,14 +901,18 @@
         away = lax.dynamic_slice_in_dim(value, (1 - side) * images, images, axis=0)
         return own, swap(away, "seq", 1, 2)
 
-    def restore(own, oth):
-        back = swap(oth, "seq", 1, 2).astype(own.dtype)
+    x_own, x_oth = exchange(patches)
+    c_own, c_oth = exchange(cotangent)
+
+    def place(own, back):
+        back = back.astype(own.dtype)
         first = jnp.where(side == 0, own, back)
         second = jnp.where(side == 0, back, own)
         return jnp.concatenate([first, second], axis=0).reshape(all_images, 1, half, width)
 
-    x_own, x_oth = exchange(patches)
-    c_own, c_oth = exchange(cotangent)
+    def restore(own, oth):
+        return place(own, swap(oth, "seq", 1, 2))
+
     across = grid_shape[:, 1]
     counts = jnp.stack([split_rows * across, (grid_shape[:, 0] - split_rows) * across], axis=0)
     count_own = jnp.where(side == 0, counts[0], counts[1])
@@ -718,28 +932,30 @@
     dn2, s2, k2, s1, k1, fc2_bias_grad, fc1_bias_grad = mlp_back(
         scal, mine, c_own, c_oth, flat(n2), hidden, slope, w, unit1, unit2
     )
-    d_middle, d_branch, d_join, ln2_gain_grad, ln2_bias_grad, proj_bias_grad, q_grad, v_grad = attend_back(
-        scal, c_own, c_oth, dn2.reshape(images, rows, width), middle, qkv, probs, w
-    )
-    st, kt, grad_own, grad_oth, ln1_gain_grad, ln1_bias_grad = tail(
-        mine, flat(n1), flat(d_join), flat(attended), flat(d_branch), x_own, x_oth, flat(d_middle), w, unit1
-    )
-    patches_grad = restore(grad_own, grad_oth)
-    vectors = (
-        ln1_gain_grad, ln1_bias_grad, jnp.concatenate([q_grad, v_grad], axis=1), proj_bias_grad, ln2_gain_grad,
-        ln2_bias_grad, fc1_bias_grad, fc2_bias_grad,
-    )
+    dn2 = dn2.reshape(images, rows, width)
     if owners == GROUP:
-        small = jnp.concatenate([v.reshape(owners, -1) for v in vectors], axis=1)
-        small = jnp.pad(small, ((0, 0), (0, 1024 - small.shape[1]))).reshape(owners, 8, 128)
-        fc2_grad, fc1_grad, qkv_grad, proj_grad, small = reduce_all(s2, k2, s1, k1, st, kt, small)
-        small = small.reshape(-1)
+        fc2_grad, fc1_grad, qkv_grad, proj_grad, sums, grad_own, back = finish(
+            scal, c_own, c_oth, dn2, middle, qkv, probs, n1, attended, x_own, x_oth, s2, k2, s1, k1,
+            fc1_bias_grad, fc2_bias_grad, w
+        )
+        patches_grad = place(grad_own, back)
+        owner = 2 * line + side
         pieces = []
-        at = 0
-        for v in vectors:
-            pieces.append(small[at : at + v.shape[1] // owners])
-            at += v.shape[1] // owners
+        for at, count in ((0, 1), (1, 1), (2, 2), (4, 1), (5, 1), (6, 1), (7, 4), (11, 1)):
+            vector = sums[at : at + count].reshape(-1)
+            pieces.append(lax.dynamic_slice_in_dim(vector, owner * count * unit1, count * unit1))
     else:
+        d_middle, d_branch, d_join, ln2_gain_grad, ln2_bias_grad, proj_bias_grad, q_grad, v_grad = attend_back(
+            scal, c_own, c_oth, dn2, middle, qkv, probs, w
+        )
+        st, kt, grad_own, grad_oth, ln1_gain_grad, ln1_bias_grad = tail(
+            mine, flat(n1), flat(d_join), flat(attended), flat(d_branch), x_own, x_oth, flat(d_middle), w, unit1
+        )
+        patches_grad = restore(grad_own, grad_oth)
+        vectors = (
+            ln1_gain_grad, ln1_bias_grad, jnp.concatenate([q_grad, v_grad], axis=1), proj_bias_grad, ln2_gain_grad,
+            ln2_bias_grad, fc1_bias_grad, fc2_bias_grad,
+        )
         fc2_grad = spread(unfold(s2, k2, line % 2, 1))
         fc1_grad = spread(unfold(s1, k1, line % 2, 2))
         tail_grad = spread(unfold(st, kt, line % 2, 2))

time: 264 us -> 232 us (0.88)
  Pallas kernels: 221 us -> 183 us
  waiting for transfers between devices: 10.4 us -> 19.7 us
    pallas_call x3 -> x1, Pallas kernels: 141 us -> 103 us  [finish(): pl.pallas_call(finish_kernel, in_specs=[smem] + [hbm] * 16 + [vmem] * 4,...]
    ppermute x4 -> x3, waiting for transfers between devices: 10.4 us -> 19.7 us  [swap(): return lax.ppermute(value, axis, [(i, i ^ bit) for i in range(size)])]
    dynamic_slice x0 -> x5, local copies, waits for them, and re-layouts: none -> 2.93 us  [shards(): lax.dynamic_slice_in_dim(vector, owner * count * unit1, count * unit1)]
    unnamed x57 -> x45, local copies, waits for them, and re-layouts: 7.07 us -> 4.63 us
  transfers between devices with their start and end apart: 4 -> 3, of which waited for: 1 -> 2; matrix products, arithmetic and copies ran while one was open for 5% -> 6% of each run, Pallas kernels for 84% -> 21%
where the time goes in v1:
time: 232 us; the launch traced here: 231 us
  Pallas kernels  183 us (79%)
  waiting for transfers between devices  19.7 us (8%)
  local copies, waits for them, and re-layouts  19.3 us (8%)
  other arithmetic  4.96 us (2%)
  starting transfers between devices  3.14 us (1%)
    pallas_call x1, Pallas kernels, finish(): pl.pallas_call(finish_kernel, in_specs=[smem] + [hbm] * 16 + [vmem] * 4,...  103 us
    pallas_call x1, Pallas kernels, mlp_back(): pl.pallas_call(mlp_back_kernel, grid_spec=pltpu.PrefetchScalarGridSpec(nu...  30.3 us
    pallas_call x1, Pallas kernels, mlp(): pl.pallas_call(mlp_kernel, grid_spec=pltpu.PrefetchScalarGridSpec(num_sca...  25.7 us
    pallas_call x1, Pallas kernels, front(): pl.pallas_call(front_kernel, grid_spec=pltpu.PrefetchScalarGridSpec(num_s...  23.8 us
    ppermute x3, waiting for transfers between devices, swap(): return lax.ppermute(value, axis, [(i, i ^ bit) for i in range(size)])  19.7 us
    reshape x8, local copies, waits for them, and re-layouts, shards(): row = lambda v: v.reshape(1, -1)  4.69 us
  transfers between devices with their start and end apart: 3, of which 2 were waited for; matrix products, arithmetic and copies ran while one was open for 6% of the time, Pallas kernels for 21%

profile of v1, /device:TPU:0, one launch (start us, length us, event | category | flops | bytes accessed | tf_op | source)
XLA Modules:
  0.0 231.2 jit_solution(9717308968627640088)
XLA Ops:
  0.7 2.5 %dynamic-slice_bitcast_fusion.2 = (bf16[3,160,768]{2,1,0:T(8,128)(2,1)S(1)}, bf16[3,160,768]{2,1,0:T(8,128)(2,1)}) fusion(bf16[6,1,160,768]{3,2,1,0:T(8,128)(2,1)} %param.18, s32[]{:T(128)S(6)} %select_n.62, s32[]{:T(128)S(6)} %select_n.61), kind=kLoop, calls=%fused_computation.6 | loop fusion | bytes 2949128 | tf_op jit(solution)/shard_map/dynamic_slice | solution.py:901
  3.2 0.0 copy-start.10
  3.2 0.0 copy-start.8
  3.2 0.0 copy-start.13
  3.2 0.0 copy-start.14
  3.2 3.0 %collective-permute-start = (bf16[3,160,768]{2,1,0:T(8,128)(2,1)S(1)}, bf16[3,160,768]{2,1,0:T(8,128)(2,1)S(1)}, u32[]{:S(2)}, u32[]{:S(2)}) collective-permute-start(bf16[3,160,768]{2,1,0:T(8,128)(2,1)S(1)} %get-tuple-element.82), channel_id=1, source_target_pairs={{0,1},{1,0},{2,3},{3,2},{4,5},{5,4},{6,7},{7,6},{8,9},{9,8},{10,11... | collective-permute-start | bytes 2211848 | tf_op jit(solution)/shard_map/ppermute | solution.py:878
  6.2 1.0 dynamic-slice_bitcast_fusion
  7.2 0.0 collective-permute-start.2
  7.3 0.1 copy.32
  7.4 0.1 copy.33
  7.5 0.1 copy.34
  7.6 0.1 copy.35
  7.7 0.1 copy.36
  7.8 0.6 reshape.104.g1_ref
  8.3 0.6 reshape.105.b1_ref
  8.9 0.6 reshape.106.qb_ref
  9.5 0.6 reshape.107.vb_ref
  10.1 0.6 reshape.108.pb_ref
  10.7 0.6 reshape.109.g2_ref
  11.3 0.6 reshape.110.b2_ref
  11.9 0.6 reshape.114.c2_ref
  12.5 0.1 stack.20
  12.5 0.6 constant_dynamic-slice_fusion.6.scal_ref
  13.1 10.4 %collective-permute-done.oth_ref.x_oth = bf16[3,160,768]{2,1,0:T(8,128)(2,1)S(1)} collective-permute-done((bf16[3,160,768]{2,1,0:T(8,128)(2,1)S(1)}, bf16[3,160,768]{2,1,0:T(8,128)(2,1)S(1)}, u32[]{:S(2)}, u32[]{:S(2)}) %collective-permute-start) | collective-permute-done | bytes 737312 | tf_op jit(solution)/shard_map/ppermute | solution.py:878
  23.5 0.9 copy-done.1
  24.4 23.8 %front.1 = (bf16[3,320,768]{2,1,0:T(8,128)(2,1)}, bf16[3,320,2304]{2,1,0:T(8,128)(2,1)}, bf16[3,12,320,320]{3,2,1,0:T(8,128)(2,1)}, bf16[3,320,768]{2,1,0:T(8,12...) custom-call(s32[3,6]{1,0:T(4,128)} %constant_dynamic-slice_fusion.6.scal_ref, ...), custom_call_target="tpu_custom_call" | custom-call | flops 6417285120 | bytes 30000000 | tf_op jit(solution)/shard_map/front/pallas_call | solution.py:120
  48.2 25.7 %mlp.1 = (bf16[960,3072]{1,0:T(8,128)(2,1)}, bf16[960,3072]{1,0:T(8,128)(2,1)}, bf16[3,160,768]{2,1,0:T(8,128)(2,1)}, bf16[3,160,768]{2,1,0:T(8,128)(2,1)}) custom-call(s32[3,6]{1,0:T(4,128)} %constant_dynamic-slice_fusion.6.scal_ref, bf16[960,768]{1,0:T(8,128)(2,1)} %bitcast.67, f32[960,768]{1,0:T(8,128)} %bitcast.62, bf16[768,3072]{1,0:T(8,128)(2,1)} %w1_ref.3, ...), custom_call_target="tpu_custom_call" | custom-call | flops 9059696640 | bytes 30000000 | tf_op jit(solution)/shard_map/mlp/pallas_call | solution.py:186
  73.9 0.8 copy-done.2
  74.7 30.3 %mlp_back.1 = (f32[960,768]{1,0:T(8,128)}, bf16[4,2,2,96,768]{4,3,2,1,0:T(8,128)(2,1)}, bf16[4,2,2,96,768]{4,3,2,1,0:T(8,128)(2,1)}, bf16[8,2,48,1536]{3,2,1,0:T...) custom-call(s32[3,6]{1,0:T(4,128)} %constant_dynamic-slice_fusion.6.scal_ref, ...), custom_call_target="tpu_custom_call" | custom-call | flops 18119393280 | bytes 35000000 | tf_op jit(solution)/shard_map/mlp_back/pallas_call | solution.py:287
  105.1 103.4 %finish.1 = (f32[96,768]{1,0:T(8,128)}, f32[24,3072]{1,0:T(8,128)}, f32[24,2304]{1,0:T(8,128)}, f32[24,768]{1,0:T(8,128)}, f32[16,768]{1,0:T(8,128)}, /*index=5*...) custom-call(s32[3,6]{1,0:T(4,128)} %constant_dynamic-slice_fusion.6.scal_ref, ...), custom_call_target="tpu_custom_call" | custom-call | tf_op jit(solution)/shard_map/finish/pallas_call | solution.py:814
  208.5 1.0 fusion.10
  209.5 0.7 slice.45
  210.3 0.8 slice.49
  211.1 0.1 collective-permute-start.1
  211.2 0.6 dynamic_slice.72
  211.8 0.6 dynamic_slice.79
  212.4 0.6 fusion.2
  213.0 0.6 fusion.4
  213.5 0.6 fusion.6
  214.1 1.8 convert_select_fusion.1
  216.0 1.8 maximum_bitcast_fusion
  217.8 9.3 %collective-permute-done.1 = bf16[3,160,768]{2,1,0:T(8,128)(2,1)S(1)} collective-permute-done((bf16[3,160,768]{2,1,0:T(8,128)(2,1)S(1)}, bf16[3,160,768]{2,1,0:T(8,128)(2,1)S(1)}, u32[]{:S(2)}, u32[]{:S(2)}) %collective-permute-start.1) | collective-permute-done | bytes 737312 | tf_op jit(solution)/shard_map/ppermute | solution.py:878
  227.0 0.1 broadcast_select_fusion.1
  227.2 1.2 maximum_bitcast_fusion.1
  228.4 0.7 copy.43
  229.1 0.6 copy.44
  229.8 0.7 copy.45
  230.5 0.7 copy.46
  (41 shorter events, 0.1 us)
Async XLA Ops:
  0.7 5.6 %copy-start = (bf16[6,1,160,768]{3,2,1,0:T(8,128)(2,1)S(1)}, bf16[6,1,160,768]{3,2,1,0:T(8,128)(2,1)}, u32[]{:S(2)}) copy-start(bf16[6,1,160,768]{3,2,1,0:T(8,128)(2,1)} %param.35) | copy-start | bytes 4423684
  3.1 4.1 %copy-start.15 = (s32[6,2]{0,1:T(2,128)S(1)}, s32[6,2]{0,1:T(2,128)}, u32[]{:S(2)}) copy-start(s32[6,2]{0,1:T(2,128)} %param.19) | copy-start | bytes 148
  3.1 4.1 %copy-start.17 = (s32[6]{0:T(128)S(1)}, s32[6]{0:T(128)}, u32[]{:S(2)}) copy-start(s32[6]{0:T(128)} %param.20) | copy-start | bytes 76
  3.1 4.2 %copy-start.19 = (s32[6]{0:T(128)S(1)}, s32[6]{0:T(128)}, u32[]{:S(2)}) copy-start(s32[6]{0:T(128)} %param.21) | copy-start | bytes 76
  3.1 4.5 %copy-start.16 = (s32[6,2]{0,1:T(2,128)S(1)}, s32[6,2]{0,1:T(2,128)}, u32[]{:S(2)}) copy-start(s32[6,2]{0,1:T(2,128)} %param.22) | copy-start | bytes 148
  3.1 4.6 %copy-start.9 = (f32[768]{0:T(1024)S(1)}, f32[768]{0:T(1024)}, u32[]{:S(2)}) copy-start(f32[768]{0:T(1024)} %param.23) | copy-start | bytes 9220
  3.2 5.2 %copy-start.10 = (f32[768]{0:T(1024)S(1)}, f32[768]{0:T(1024)}, u32[]{:S(2)}) copy-start(f32[768]{0:T(1024)} %param.24) | copy-start | bytes 9220
  3.2 5.8 %copy-start.8 = (f32[1536]{0:T(1024)S(1)}, f32[1536]{0:T(1024)}, u32[]{:S(2)}) copy-start(f32[1536]{0:T(1024)} %param.26) | copy-start | bytes 18436
  3.2 6.9 %copy-start.11 = (f32[768]{0:T(1024)S(1)}, f32[768]{0:T(1024)}, u32[]{:S(2)}) copy-start(f32[768]{0:T(1024)} %param.28) | copy-start | bytes 9220
  3.2 7.5 %copy-start.12 = (f32[768]{0:T(1024)S(1)}, f32[768]{0:T(1024)}, u32[]{:S(2)}) copy-start(f32[768]{0:T(1024)} %param.29) | copy-start | bytes 9220
  3.2 8.1 %copy-start.13 = (f32[768]{0:T(1024)S(1)}, f32[768]{0:T(1024)}, u32[]{:S(2)}) copy-start(f32[768]{0:T(1024)} %param.30) | copy-start | bytes 9220
  3.2 8.7 %copy-start.14 = (f32[768]{0:T(1024)S(1)}, f32[768]{0:T(1024)}, u32[]{:S(2)}) copy-start(f32[768]{0:T(1024)} %param.34) | copy-start | bytes 9220
  3.2 20.3 %collective-permute-start = (bf16[3,160,768]{2,1,0:T(8,128)(2,1)S(1)}, bf16[3,160,768]{2,1,0:T(8,128)(2,1)S(1)}, u32[]{:S(2)}, u32[]{:S(2)}) collective-permute-start(bf16[3,160,768]{2,1,0:T(8,128)(2,1)S(1)} %get-tuple-element.82), channel_id=1, source_target_pairs={{0,1},{1,0},{2,3},{3,2},{4,5},{5,4},{6,7},{7,6},{8,9},{9,8},{10,11... | collective-permute-start | bytes 2211848 | tf_op jit(solution)/shard_map/ppermute | solution.py:878
  7.2 66.7 %collective-permute-start.2 = (bf16[3,160,768]{2,1,0:T(8,128)(2,1)S(1)}, bf16[3,160,768]{2,1,0:T(8,128)(2,1)S(1)}, u32[]{:S(2)}, u32[]{:S(2)}) collective-permute-start(bf16[3,160,768]{2,1,0:T(8,128)(2,1)S(1)} %get-tuple-element.78), channel_id=1, source_target_pairs={{0,1},{1,0},{2,3},{3,2},{4,5},{5,4},{6,7},{7,6},{8,9},{9,8},{10,11... | collective-permute-start | bytes 2211848 | tf_op jit(solution)/shard_map/ppermute | solution.py:878
  23.5 0.9 copy-start.1
  73.9 0.9 copy-start.2
  105.1 106.0 %copy-start.18 = (bf16[3,160,768]{2,1,0:T(8,128)(2,1)S(1)}, bf16[3,160,768]{2,1,0:T(8,128)(2,1)}, u32[]{:S(2)}) copy-start(bf16[3,160,768]{2,1,0:T(8,128)(2,1)} %get-tuple-element.41) | copy-start | bytes 2211844
  211.1 16.0 %collective-permute-start.1 = (bf16[3,160,768]{2,1,0:T(8,128)(2,1)S(1)}, bf16[3,160,768]{2,1,0:T(8,128)(2,1)S(1)}, u32[]{:S(2)}, u32[]{:S(2)}) collective-permute-start(bf16[3,160,768]{2,1,0:T(8,128)(2,1)S(1)} %copy-done.18), channel_id=1, source_target_pairs={{0,1},{1,0},{2,3},{3,2},{4,5},{5,4},{6,7},{7,6},{8,9},{9,8},{10,11... | collective-permute-start | bytes 2211848 | tf_op jit(solution)/shard_map/ppermute | solution.py:878
  216.0 11.1 %copy-start.3 = (bf16[3,160,768]{2,1,0:T(8,128)(2,1)S(1)}, bf16[3,160,768]{2,1,0:T(8,128)(2,1)}, u32[]{:S(2)}) copy-start(bf16[3,160,768]{2,1,0:T(8,128)(2,1)} %get-tuple-element.40) | copy-start | bytes 2211844
  227.1 1.3 copy-start.6
  227.2 2.0 copy-start.7
  227.2 2.6 %copy-start.5 = (f32[24,3072]{1,0:T(8,128)S(1)}, f32[24,3072]{1,0:T(8,128)}, u32[]{:S(2)}) copy-start(f32[24,3072]{1,0:T(8,128)} %get-tuple-element.124) | copy-start | bytes 884740
  227.2 3.3 %copy-start.4 = (f32[96,768]{1,0:T(8,128)S(1)}, f32[96,768]{1,0:T(8,128)}, u32[]{:S(2)}) copy-start(f32[96,768]{1,0:T(8,128)} %get-tuple-element.126) | copy-start | bytes 884740
